TPU v7x, 32 devices: a whole 2x2x4 slice. The times are simulated.
32 devices in a mesh: ctx: 8 (over y, x, core), head: 4 (over z).
Axes of the slice: x: 2, y: 2, z: 4, core: 2. Of those that a mesh axis runs over, the one named last changes fastest.
Arguments:
- queries: bfloat16 [2048, 4096], P('ctx', 'head'), may hold values from -6 to 6
- key_rows: bfloat16 [2048, 4096], P('ctx', 'head'), may hold values from -6 to 6
- value_rows: bfloat16 [2048, 4096], P('ctx', 'head'), may hold values from -6 to 6
- out_weight: bfloat16 [4096, 4096], P('head'), may hold values from -0.125 to 0.125
- cotangent: bfloat16 [2048, 4096], P('ctx', 'head'), may hold values from -6 to 6
Outputs:
- mixed: bfloat16 [2048, 4096], P('ctx', 'head')
- grad_queries: bfloat16 [2048, 4096], P('ctx', 'head')
- grad_keys: bfloat16 [2048, 4096], P('ctx', 'head')
- grad_values: bfloat16 [2048, 4096], P('ctx', 'head')
- grad_out_weight: float32 [4096, 4096], P('head', 'ctx')
All inputs are finite; a program needn't handle non-finite values.
Results may differ from a plain program's by a relative error of at most 0.0052.
Values may be sent and summed in bfloat16 or wider, within the bound.
No kernel may reach another device: no remote copies, remote signals or barrier semaphores. Data moves between devices by JAX's collectives and lax.ppermute only.
A program may use at most 64 MiB of HBM per device.

v0:
```python
import functools

import jax
import jax.numpy as jnp
from jax import lax
from jax.experimental import pallas as pl
from jax.experimental.pallas import tpu as pltpu
from jax.sharding import PartitionSpec as P


HEAD_DIM = 128

epsilon = 1e-06


bf16 = jnp.bfloat16
f32 = jnp.float32
VMEM = pl.BlockSpec(memory_space=pltpu.VMEM)
GRANT = 24 << 20


def mm(a, b, da, db):
    return lax.dot_general(a, b, (((da,), (db,)), ((), ())), preferred_element_type=f32)


def split(x):
    high = x.astype(bf16)
    return high, (x - high.astype(f32)).astype(bf16)


def head(h):
    return slice(h * HEAD_DIM, (h + 1) * HEAD_DIM)


def below(n):
    return lax.broadcasted_iota(jnp.int32, (n, n), 0) >= lax.broadcasted_iota(jnp.int32, (n, n), 1)


def array(shape, dtype):
    return jax.ShapeDtypeStruct(shape, dtype)


def kernel_call(kernel, *args, **settings):
    return pl.pallas_call(kernel, compiler_params=pltpu.CompilerParams(vmem_limit_bytes=GRANT), **settings)(*args)


def call(kernel, outs, *args):
    return kernel_call(
        kernel, *args, out_shape=outs, in_specs=[VMEM] * len(args), out_specs=jax.tree.map(lambda _: VMEM, outs)
    )


def state_kernel(k, v, out):
    for h in range(k.shape[1] // HEAD_DIM):
        out[head(h), :] = mm(k[:, head(h)], v[:, head(h)], 0, 0)


def intra_kernel(q, k, v, out):
    keep = below(q.shape[0])
    for h in range(q.shape[1] // HEAD_DIM):
        scores = jnp.where(keep, mm(q[:, head(h)], k[:, head(h)], 1, 1), 0.0).astype(bf16)
        out[:, head(h)] = mm(scores, v[:, head(h)], 1, 0)


def row_scale_of(attended):
    return lax.rsqrt(jnp.mean(attended * attended, axis=-1, keepdims=True) + epsilon)


def norm_kernel(q, intra, prefix, attended, normed):
    for h in range(q.shape[1] // HEAD_DIM):
        high, low = split(prefix[head(h), :])
        query = q[:, head(h)]
        value = intra[:, head(h)] + mm(query, high, 1, 0) + mm(query, low, 1, 0)
        attended[:, head(h)] = value
        normed[:, head(h)] = (value * row_scale_of(value)).astype(bf16)


def pieces_kernel(count, rounded, _, normed, *refs):
    weights, outs = refs[:count], refs[count:]
    for n in range(count):
        value = mm(normed[...], weights[n][...], 1, 0)
        outs[n][...] = value
        if rounded:
            outs[count + n][...] = value.astype(bf16)


def upstream_kernel(count, _, *refs):
    slots, weights, out = refs[:count], refs[count : 2 * count], refs[2 * count]
    value = mm(slots[0][...], weights[0][...], 1, 1)
    for n in range(1, count):
        value = value + mm(slots[n][...], weights[n][...], 1, 1)
    out[...] = value


def finish_kernel(count, _, *refs):
    slots, weights = refs[:count], refs[count : 2 * count]
    so_far, attended, q, d_out, grad_out = refs[2 * count :]
    upstream = so_far[...]
    for n in range(count):
        upstream = upstream + mm(slots[n][...], weights[n][...], 1, 1)
    for h in range(d_out.shape[1] // HEAD_DIM):
        value, up = attended[:, head(h)], upstream[:, head(h)]
        scale = row_scale_of(value)
        unit = value * scale
        grad = scale * (up - unit * jnp.mean(up * unit, axis=-1, keepdims=True))
        grad = grad.astype(bf16)
        d_out[:, head(h)] = grad
        grad_out[head(h), :] = mm(q[:, head(h)], grad, 0, 0)


def back_kernel(q, k, v, d, prefix, grad_q, part_k, part_v):
    keep = below(q.shape[0])
    for h in range(q.shape[1] // HEAD_DIM):
        qh, kh, vh, dh = q[:, head(h)], k[:, head(h)], v[:, head(h)], d[:, head(h)]
        high, low = split(prefix[head(h), :])
        scores = jnp.where(keep, mm(qh, kh, 1, 1), 0.0).astype(bf16)
        back = jnp.where(keep, mm(dh, vh, 1, 1), 0.0).astype(bf16)
        grad_q[:, head(h)] = (mm(back, kh, 1, 0) + mm(dh, high, 1, 1) + mm(dh, low, 1, 1)).astype(bf16)
        part_k[:, head(h)] = mm(back, qh, 0, 0)
        part_v[:, head(h)] = mm(scores, dh, 0, 0)


def suffix_kernel(k, v, part_k, part_v, suffix, grad_k, grad_v):
    for h in range(k.shape[1] // HEAD_DIM):
        high, low = split(suffix[head(h), :])
        kh, vh = k[:, head(h)], v[:, head(h)]
        grad_k[:, head(h)] = (part_k[:, head(h)] + mm(vh, high, 1, 1) + mm(vh, low, 1, 1)).astype(bf16)
        grad_v[:, head(h)] = (part_v[:, head(h)] + mm(kh, high, 1, 0) + mm(kh, low, 1, 0)).astype(bf16)


def weight_grad_kernel(count, adds, _, *refs):
    rows, cols = refs[:count], refs[count : 2 * count]
    out = refs[-1]
    value = mm(rows[0][...], cols[0][...], 0, 0)
    for n in range(1, count):
        value = value + mm(rows[n][...], cols[n][...], 0, 0)
    if adds:
        value = value + refs[2 * count][...].astype(f32)
    out[...] = value.astype(out.dtype)


def flipped(size, mask):
    return [(i, i ^ mask) for i in range(size)]


def shifted(size, by):
    return [(i, (i + by) % size) for i in range(size)]


def exclusive_sum(block, position, size, upward):
    total = block
    outer = jnp.zeros_like(block)
    mask = 1
    while mask < size:
        sent = total if mask == 1 else total.astype(bf16)
        other = lax.ppermute(sent, "ctx", flipped(size, mask))
        other = other.astype(f32)
        upper = (position & mask) != 0
        take = upper if upward else jnp.logical_not(upper)
        outer = outer + jnp.where(take, other, 0.0)
        total = total + other
        mask *= 2
    return outer


def make_body(n_ctx, n_head):
    pair = min(2, n_ctx)
    chips = n_ctx // pair

    def body(queries, key_rows, value_rows, out_weight, cotangent):
        length, width = queries.shape
        heads_here = width // HEAD_DIM
        model = out_weight.shape[1]
        part = model // n_head
        chip_cols = model // chips
        own_cols = chip_cols // pair
        tiles = 2 if heads_here % 2 == 0 else 1
        position = lax.axis_index("ctx")
        place = lax.axis_index("head")
        place_at = place.reshape(1).astype(jnp.int32)

        slots = [cotangent]
        for r in range(1, n_head):
            slots.append(lax.ppermute(cotangent, "head", shifted(n_head, r)))

        block_state = call(state_kernel, array((width, HEAD_DIM), f32), key_rows, value_rows)
        intra = call(intra_kernel, array((length, width), f32), queries, key_rows, value_rows)
        prefix = exclusive_sum(block_state, position, n_ctx, True)
        attended, normed = call(
            norm_kernel, (array((length, width), f32), array((length, width), bf16)), queries, intra, prefix
        )

        def pieces(steps, rounded):
            steps = tuple(steps)
            tile = part // tiles
            blocks = [
                pl.BlockSpec(
                    (width, tile),
                    functools.partial(lambda s, i, at: (0, lax.rem(at[0] + s, n_head) * tiles + i), s),
                )
                for s in steps
            ]
            out = pl.BlockSpec((length, tile), lambda i, at: (0, i))
            copies = 2 if rounded else 1
            got = kernel_call(
                functools.partial(pieces_kernel, len(steps), rounded),
                place_at,
                normed,
                *([out_weight] * len(steps)),
                out_shape=[array((length, part), f32)] * len(steps)
                + [array((length, part), bf16)] * (len(steps) if rounded else 0),
                grid_spec=pltpu.PrefetchScalarGridSpec(
                    num_scalar_prefetch=1,
                    grid=(tiles,),
                    in_specs=[pl.BlockSpec((length, width), lambda i, at: (0, 0))] + blocks,
                    out_specs=[out] * (len(steps) * copies),
                ),
            )
            wide = dict(zip(steps, got[: len(steps)]))
            return wide, dict(zip(steps, got[len(steps) :]))

        first = sorted({1, n_head - 1} - {0}) if n_head > 1 else []
        wide, narrow = pieces(first, True) if first else ({}, {})
        rest = [s for s in range(n_head) if s not in first]
        wide_rest, _ = pieces(rest, False)
        wide = {**wide, **wide_rest}
        right = left = None
        for r in range(1, n_head):
            if r == 1:
                send_right, send_left = narrow[n_head - 1], narrow[1]
            else:
                send_right = (wide[n_head - r] + right).astype(bf16)
                send_left = (wide[r] + left).astype(bf16)
            right = lax.ppermute(
                send_right, "head", [(i, i + 1) for i in range(min(r, n_head - 1))]
            ).astype(f32)
            left = lax.ppermute(send_left, "head", [(i, i - 1) for i in range(max(1, n_head - r), n_head)]).astype(f32)
        mixed = wide[0] if right is None else wide[0] + right + left
        mixed = mixed.astype(bf16)

        perms = [flipped(n_ctx, m) for m in range(pair, n_ctx, pair)]
        rows = [normed]
        for perm in perms:
            rows.append(lax.ppermute(normed, "ctx", perm))

        def weight_specs(which):
            return [
                pl.BlockSpec(
                    (width // tiles, part),
                    functools.partial(lambda r, i, at: (i, lax.rem(at[0] + n_head - r, n_head)), r),
                )
                for r in which
            ]

        late = [n_head // 2] if n_head > 1 else []
        early = [r for r in range(n_head) if r not in late]
        slot_spec = pl.BlockSpec((length, part), lambda i, at: (0, 0))
        tile_spec = pl.BlockSpec((length, width // tiles), lambda i, at: (0, i))
        so_far = kernel_call(
            functools.partial(upstream_kernel, len(early)),
            place_at,
            *[slots[r] for r in early],
            *([out_weight] * len(early)),
            out_shape=array((length, width), f32),
            grid_spec=pltpu.PrefetchScalarGridSpec(
                num_scalar_prefetch=1,
                grid=(tiles,),
                in_specs=[slot_spec] * len(early) + weight_specs(early),
                out_specs=tile_spec,
            ),
        )
        d_attended, grad_block = kernel_call(
            functools.partial(finish_kernel, len(late)),
            place_at,
            *[slots[r] for r in late],
            *([out_weight] * len(late)),
            so_far,
            attended,
            queries,
            out_shape=(array((length, width), bf16), array((width, HEAD_DIM), f32)),
            grid_spec=pltpu.PrefetchScalarGridSpec(
                num_scalar_prefetch=1,
                grid=(tiles,),
                in_specs=[slot_spec] * len(late) + weight_specs(late) + [tile_spec] * 3,
                out_specs=(tile_spec, pl.BlockSpec((width // tiles, HEAD_DIM), lambda i, at: (i, 0))),
            ),
        )

        def columns_of(chip):
            if chip_cols == part:
                slot = lax.rem(place - chip + n_head, n_head)
                got = slots[0]
                for r in range(1, n_head):
                    got = jnp.where(slot == r, slots[r], got)
                return got
            stacked = jnp.stack(slots)
            if chip_cols < part:
                start = chip * chip_cols
                slot = lax.rem(place - start // part + n_head, n_head)
                at = (slot, 0, lax.rem(start, part))
                return lax.dynamic_slice(stacked, at, (1, length, chip_cols))[0]
            each = chip_cols // part
            taken = []
            for n in range(each):
                slot = lax.rem(place - (chip * each + n) + n_head, n_head)
                taken.append(lax.dynamic_index_in_dim(stacked, slot, 0, keepdims=False))
            return jnp.concatenate(taken, axis=1)

        cols = [columns_of(position // pair)]
        for n, perm in enumerate(perms):
            piece = columns_of((position ^ ((n + 1) * pair)) // pair)
            cols.append(lax.ppermute(piece, "ctx", perm))

        wide_out = array((length, width), f32)
        narrow_out = array((length, width), bf16)
        grad_q, part_k, part_v = call(
            back_kernel, (narrow_out, wide_out, wide_out), queries, key_rows, value_rows, d_attended, prefix
        )
        suffix = exclusive_sum(grad_block, position, n_ctx, False)
        grad_k, grad_v = call(suffix_kernel, (narrow_out, narrow_out), key_rows, value_rows, part_k, part_v, suffix)

        def weight_grad(core, dtype, *extra):
            row_tiles = 2 if width % (2 * HEAD_DIM) == 0 else 1
            out = pl.BlockSpec((width // row_tiles, own_cols), lambda i, at: (i, 0))
            return kernel_call(
                functools.partial(weight_grad_kernel, len(rows), len(extra)),
                core.reshape(1).astype(jnp.int32),
                *rows,
                *cols,
                *extra,
                out_shape=array((width, own_cols), dtype),
                grid_spec=pltpu.PrefetchScalarGridSpec(
                    num_scalar_prefetch=1,
                    grid=(row_tiles,),
                    in_specs=[pl.BlockSpec((length, width // row_tiles), lambda i, at: (0, i))] * len(rows)
                    + [pl.BlockSpec((length, own_cols), lambda i, at: (0, at[0]))] * len(cols)
                    + [out] * len(extra),
                    out_specs=out,
                ),
            )

        core = lax.rem(position, pair)
        if pair > 1:
            sent = weight_grad(1 - core, bf16)
            other = lax.ppermute(sent, "ctx", flipped(n_ctx, 1))
            grad_out_weight = weight_grad(core, f32, other)
        else:
            grad_out_weight = weight_grad(core, f32)
        return mixed, grad_q, grad_k, grad_v, grad_out_weight

    return body


def solution(mesh):
    n_ctx, n_head = mesh.shape["ctx"], mesh.shape["head"]
    body = make_body(n_ctx, n_head)

    return jax.shard_map(
        body,
        mesh=mesh,
        in_specs=(P("ctx", "head"),) * 3 + (P("head", None), P("ctx", "head")),
        out_specs=(P("ctx", "head"),) * 4 + (P("head", "ctx"),),
        check_vma=False,
    )
```

profile of v0, /device:TPU:0, one launch (start us, length us, event | category | flops | bytes accessed | tf_op | source)
XLA Modules:
  0.0 154.0 jit_solution(13605861224124683612)
XLA Ops:
  3.6 1.5 collective-permute-done
  5.2 2.9 %collective-permute-start.1 = (bf16[1024,128]{1,0:T(8,128)(2,1)S(1)}, bf16[1024,128]{1,0:T(8,128)(2,1)S(1)}, u32[]{:S(2)}, u32[]{:S(2)}) collective-permute-start(bf16[1024,128]{1,0:T(8,128)(2,1)S(1)} %get-tuple-element.37), channel_id=1, source_target_pairs={{0,8},{4,12},{8,0},{12,4},{16,24},{20,28},{24,16},{28,20},{1,9},{5... | collective-permute-start | bytes 786440 | tf_op jit(solution)/shard_map/ppermute | solution.py:156
  8.2 6.6 %collective-permute-done.1 = bf16[1024,128]{1,0:T(8,128)(2,1)S(1)} collective-permute-done((bf16[1024,128]{1,0:T(8,128)(2,1)S(1)}, bf16[1024,128]{1,0:T(8,128)(2,1)S(1)}, u32[]{:S(2)}, u32[]{:S(2)}) %collective-permute-start.1) | collective-permute-done | bytes 262176 | tf_op jit(solution)/shard_map/ppermute | solution.py:156
  14.8 1.8 %collective-permute-start.2 = (bf16[1024,128]{1,0:T(8,128)(2,1)S(1)}, bf16[1024,128]{1,0:T(8,128)(2,1)}, u32[]{:S(2)}, u32[]{:S(2)}) collective-permute-start(bf16[1024,128]{1,0:T(8,128)(2,1)S(1)} %fusion.2), channel_id=1, source_target_pairs={{0,16},{4,20},{8,24},{12,28},{16,0},{20,4},{24,8},{28,12},{1,17},{... | collective-permute-start | bytes 786440 | tf_op jit(solution)/shard_map/ppermute | solution.py:156
  16.7 2.6 %collective-permute-start.9 = (bf16[256,1024]{1,0:T(8,128)(2,1)}, bf16[256,1024]{1,0:T(8,128)(2,1)S(1)}, u32[]{:S(2)}, u32[]{:S(2)}) collective-permute-start(bf16[256,1024]{1,0:T(8,128)(2,1)} %refs_0_.5), channel_id=1, source_target_pairs={{0,2},{1,3},{2,0},{3,1},{4,6},{5,7},{6,4},{7,5},{8,10},{9,11},{10,... | collective-permute-start | bytes 1572872 | tf_op jit(solution)/shard_map/ppermute | solution.py:184
  19.2 1.6 %collective-permute-start.10 = (bf16[256,1024]{1,0:T(8,128)(2,1)}, bf16[256,1024]{1,0:T(8,128)(2,1)}, u32[]{:S(2)}, u32[]{:S(2)}) collective-permute-start(bf16[256,1024]{1,0:T(8,128)(2,1)} %refs_0_.5), channel_id=1, source_target_pairs={{0,1},{1,2},{2,3},{3,0},{4,5},{5,6},{6,7},{7,4},{8,9},{9,10},{10,1... | collective-permute-start | bytes 1572872 | tf_op jit(solution)/shard_map/ppermute | solution.py:184
  20.8 2.2 %collective-permute-start.11 = (bf16[256,1024]{1,0:T(8,128)(2,1)}, bf16[256,1024]{1,0:T(8,128)(2,1)}, u32[]{:S(2)}, u32[]{:S(2)}) collective-permute-start(bf16[256,1024]{1,0:T(8,128)(2,1)} %refs_0_.5), channel_id=1, source_target_pairs={{0,3},{1,0},{2,1},{3,2},{4,7},{5,4},{6,5},{7,6},{8,11},{9,8},{10,9... | collective-permute-start | bytes 1572872 | tf_op jit(solution)/shard_map/ppermute | solution.py:184
  28.8 3.4 %copy-done = bf16[1024,4096]{1,0:T(8,128)(2,1)S(1)} copy-done((bf16[1024,4096]{1,0:T(8,128)(2,1)S(1)}, bf16[1024,4096]{1,0:T(8,128)(2,1)}, u32[]{:S(2)}) %copy-start) | copy-done | bytes 8388632
  32.2 2.1 %shard_map.96 = (f32[256,1024]{1,0:T(8,128)S(1)}, f32[256,1024]{1,0:T(8,128)S(1)}, bf16[256,1024]{1,0:T(8,128)(2,1)S(1)}, bf16[256,1024]{1,0:T(8,128)(2,1)S(1)}) custom-call(s32[1]{0:T(128)} %bitcast._, bf16[256,1024]{1,0:T(8,128)(2,1)S(1)} %get-tuple-element.20.normed.refs_0_, bf16[1024,4096]{1,0:T(8,128)(2,1)S(1)} %copy-done, bf16[1024,4096]{1,0:T(8,128)(2,1)S(1)} %copy-done), custom_call_target="tpu_custom_call" | custom-call | tf_op jit(solution)/shard_map/pallas_call | solution.py:44
  34.3 1.7 %collective-permute-start.3 = (bf16[256,1024]{1,0:T(8,128)(2,1)S(1)}, bf16[256,1024]{1,0:T(8,128)(2,1)S(1)}, u32[]{:S(2)}, u32[]{:S(2)}) collective-permute-start(bf16[256,1024]{1,0:T(8,128)(2,1)S(1)} %get-tuple-element.24), channel_id=1, source_target_pairs={{0,1},{4,5},{8,9},{12,13},{16,17},{20,21},{24,25},{28,29}} | collective-permute-start | bytes 1572872 | tf_op jit(solution)/shard_map/ppermute | solution.py:234
  36.7 17.5 %collective-permute-done.9.refs_0_ = bf16[256,1024]{1,0:T(8,128)(2,1)S(1)} collective-permute-done((bf16[256,1024]{1,0:T(8,128)(2,1)}, bf16[256,1024]{1,0:T(8,128)(2,1)S(1)}, u32[]{:S(2)}, u32[]{:S(2)}) %collective-permute-start.9) | collective-permute-done | bytes 524320 | tf_op jit(solution)/shard_map/ppermute | solution.py:184
  54.8 1.4 select_select_fusion
  56.2 1.6 %collective-permute-start.18 = (bf16[256,1024]{1,0:T(8,128)(2,1)S(1)}, bf16[256,1024]{1,0:T(8,128)(2,1)S(1)}, u32[]{:S(2)}, u32[]{:S(2)}) collective-permute-start(bf16[256,1024]{1,0:T(8,128)(2,1)S(1)} %get-tuple-element.41), channel_id=1, source_target_pairs={{0,8},{4,12},{8,0},{12,4},{16,24},{20,28},{24,16},{28,20},{1,9},{5... | collective-permute-start | bytes 1572872 | tf_op jit(solution)/shard_map/ppermute | solution.py:312
  58.3 3.4 %copy-done.1 = bf16[1024,4096]{1,0:T(8,128)(2,1)S(1)} copy-done((bf16[1024,4096]{1,0:T(8,128)(2,1)S(1)}, bf16[1024,4096]{1,0:T(8,128)(2,1)}, u32[]{:S(2)}) %copy-start.1) | copy-done | bytes 8388632
  61.7 3.7 %shard_map.97.refs_2_ = f32[256,1024]{1,0:T(8,128)S(1)} custom-call(s32[1]{0:T(128)} %bitcast._, bf16[256,1024]{1,0:T(8,128)(2,1)S(1)} %copy-done.11, bf16[256,1024]{1,0:T(8,128)(2,1)} %collective-permute-done.10.refs_1_, bf16[256,1024]{1,0:T(8,128)(2,1)} %collective-permute-done.11.refs_2_, bf16[1024,4096]{1,0:T(8,128)(2,1)S(1)} %copy-done.1, ...), custom_call_target="tpu_custom_call" | custom-call | tf_op jit(solution)/shard_map/pallas_call | solution.py:44
  65.4 2.4 %shard_map.98 = (bf16[256,1024]{1,0:T(8,128)(2,1)S(1)}, f32[1024,128]{1,0:T(8,128)S(1)}) custom-call(s32[1]{0:T(128)} %bitcast._, bf16[256,1024]{1,0:T(8,128)(2,1)S(1)} %collective-permute-done.9.refs_0_, bf16[1024,4096]{1,0:T(8,128)(2,1)S(1)} %copy-done.2, f32[256,1024]{1,0:T(8,128)S(1)} %shard_map.97.refs_2_, f32[256,1024]{1,0:T(8,128)S(1)} %get-tuple-element.27.refs_3_, ...), custom_call_target="tpu_custom_call" | custom-call | tf_op jit(solution)/shard_map/pallas_call | solution.py:44
  68.6 1.9 %shard_map.95 = (f32[256,1024]{1,0:T(8,128)S(1)}, f32[256,1024]{1,0:T(8,128)S(1)}) custom-call(s32[1]{0:T(128)} %bitcast._, bf16[256,1024]{1,0:T(8,128)(2,1)S(1)} %get-tuple-element.20.normed.refs_0_, bf16[1024,4096]{1,0:T(8,128)(2,1)S(1)} %copy-done.2, bf16[1024,4096]{1,0:T(8,128)(2,1)S(1)} %copy-done.2), custom_call_target="tpu_custom_call" | custom-call | tf_op jit(solution)/shard_map/pallas_call | solution.py:44
  70.6 1.6 %collective-permute-start.20 = (bf16[256,1024]{1,0:T(8,128)(2,1)S(1)}, bf16[256,1024]{1,0:T(8,128)(2,1)S(1)}, u32[]{:S(2)}, u32[]{:S(2)}) collective-permute-start(bf16[256,1024]{1,0:T(8,128)(2,1)S(1)} %get-tuple-element.39), channel_id=1, source_target_pairs={{0,24},{4,28},{8,16},{12,20},{16,8},{20,12},{24,0},{28,4},{1,25},{... | collective-permute-start | bytes 1572872 | tf_op jit(solution)/shard_map/ppermute | solution.py:312
  72.2 1.5 collective-permute-start.15
  77.1 1.5 collective-permute-start.17
  78.6 1.5 collective-permute-start.7
  81.1 5.4 %collective-permute-done.20.refs_7_ = bf16[256,1024]{1,0:T(8,128)(2,1)S(1)} collective-permute-done((bf16[256,1024]{1,0:T(8,128)(2,1)S(1)}, bf16[256,1024]{1,0:T(8,128)(2,1)S(1)}, u32[]{:S(2)}, u32[]{:S(2)}) %collective-permute-start.20) | collective-permute-done | bytes 524320 | tf_op jit(solution)/shard_map/ppermute | solution.py:312
  87.8 10.0 %collective-permute-done.15.refs_1_ = bf16[256,1024]{1,0:T(8,128)(2,1)} collective-permute-done((bf16[256,1024]{1,0:T(8,128)(2,1)S(1)}, bf16[256,1024]{1,0:T(8,128)(2,1)}, u32[]{:S(2)}, u32[]{:S(2)}) %collective-permute-start.15) | collective-permute-done | bytes 524320 | tf_op jit(solution)/shard_map/ppermute | solution.py:244
  97.8 12.2 %collective-permute-start.4 = (bf16[256,1024]{1,0:T(8,128)(2,1)}, bf16[256,1024]{1,0:T(8,128)(2,1)S(1)}, u32[]{:S(2)}, u32[]{:S(2)}) collective-permute-start(bf16[256,1024]{1,0:T(8,128)(2,1)} %get-tuple-element.43), channel_id=1, source_target_pairs={{0,1},{1,2},{4,5},{5,6},{8,9},{9,10},{12,13},{13,14},{16,17},{17,1... | collective-permute-start | bytes 1572872 | tf_op jit(solution)/shard_map/ppermute | solution.py:234
  113.2 3.5 %shard_map.101 = bf16[1024,512]{1,0:T(8,128)(2,1)} custom-call(s32[1]{0:T(128)} %bitcast.2._, bf16[256,1024]{1,0:T(8,128)(2,1)S(1)} %get-tuple-element.20.normed.refs_0_, bf16[256,1024]{1,0:T(8,128)(2,1)} %collective-permute-done.15.refs_1_, bf16[256,1024]{1,0:T(8,128)(2,1)} %collective-permute-done.16.refs_2_, ...), custom_call_target="tpu_custom_call" | custom-call | tf_op jit(solution)/shard_map/pallas_call | solution.py:44
  116.8 1.8 %fusion.5 = bf16[1024,128]{1,0:T(8,128)(2,1)} fusion(f32[1024,128]{1,0:T(8,128)} %get-tuple-element.36, bf16[1024,128]{1,0:T(8,128)(2,1)S(1)} %collective-permute-done.13), kind=kLoop, calls=%fused_computation.14 | loop fusion | flops 393216 | bytes 1048576 | tf_op jit(solution)/shard_map/convert_element_type | solution.py:155
  119.1 2.3 %add_convert_fusion.1 = bf16[256,1024]{1,0:T(8,128)(2,1)} fusion(f32[256,1024]{1,0:T(8,128)} %copy-done.25, bf16[256,1024]{1,0:T(8,128)(2,1)} %collective-permute-done.7), kind=kLoop, calls=%fused_computation.1 | loop fusion | flops 786432 | bytes 2097152 | tf_op jit(solution)/shard_map/convert_element_type | solution.py:233
  123.7 13.6 %collective-permute-start.5 = (bf16[256,1024]{1,0:T(8,128)(2,1)}, bf16[256,1024]{1,0:T(8,128)(2,1)}, u32[]{:S(2)}, u32[]{:S(2)}) collective-permute-start(bf16[256,1024]{1,0:T(8,128)(2,1)} %add_convert_fusion.3), channel_id=1, source_target_pairs={{0,1},{1,2},{2,3},{4,5},{5,6},{6,7},{8,9},{9,10},{10,11},{12,13},{... | collective-permute-start | bytes 1572872 | tf_op jit(solution)/shard_map/ppermute | solution.py:234
  138.3 3.5 %shard_map.99 = (bf16[256,1024]{1,0:T(8,128)(2,1)}, f32[256,1024]{1,0:T(8,128)S(1)}, f32[256,1024]{1,0:T(8,128)S(1)}) custom-call(bf16[256,1024]{1,0:T(8,128)(2,1)S(1)} %copy-done.10, bf16[256,1024]{1,0:T(8,128)(2,1)S(1)} %copy-done.5, bf16[256,1024]{1,0:T(8,128)(2,1)S(1)} %copy-done.8, bf16[256,1024]{1,0:T(8,128)(2,1)S(1)} %copy-done.27, ...), custom_call_target="tpu_custom_call" | custom-call | tf_op jit(solution)/shard_map/pallas_call | solution.py:44
  143.1 1.7 %shard_map.100 = (bf16[256,1024]{1,0:T(8,128)(2,1)}, bf16[256,1024]{1,0:T(8,128)(2,1)}) custom-call(bf16[256,1024]{1,0:T(8,128)(2,1)S(1)} %copy-done.5, bf16[256,1024]{1,0:T(8,128)(2,1)S(1)} %copy-done.8, f32[256,1024]{1,0:T(8,128)S(1)} %get-tuple-element.30.part_k, f32[256,1024]{1,0:T(8,128)S(1)} %get-tuple-element.31.part_v, f32[1024,128]{1,0:T(8,128)S(1)} %fusion.4.suffix), custom_call_target="tpu_custom_call" | custom-call | tf_op jit(solution)/shard_map/pallas_call | solution.py:44
  147.9 3.8 %shard_map.102 = f32[1024,512]{1,0:T(8,128)} custom-call(s32[1]{0:T(128)} %bitcast.1._, bf16[256,1024]{1,0:T(8,128)(2,1)S(1)} %get-tuple-element.20.normed.refs_0_, bf16[256,1024]{1,0:T(8,128)(2,1)} %collective-permute-done.15.refs_1_, bf16[256,1024]{1,0:T(8,128)(2,1)} %collective-permute-done.16.refs_2_, bf16[256,1024]{1,0:T(8,128)(2,1)} %collective-permute-done.17.refs_3_, ...), custom_call_target="tpu_custom_call" | custom-call | tf_op jit(solution)/shard_map/pallas_call | solution.py:44
  151.7 2.2 %add_convert_fusion = bf16[256,1024]{1,0:T(8,128)(2,1)} fusion(bf16[256,1024]{1,0:T(8,128)(2,1)} %collective-permute-done.8, f32[256,1024]{1,0:T(8,128)S(1)} %copy-done.22, bf16[256,1024]{1,0:T(8,128)(2,1)} %collective-permute-done.5), kind=kLoop, calls=%fused_computation | loop fusion | flops 1310720 | bytes 2621440 | tf_op jit(solution)/shard_map/convert_element_type | solution.py:239
  (92 shorter events, 28.5 us)
Async XLA Ops:
  2.7 25.5 %copy-start.10 = (bf16[256,1024]{1,0:T(8,128)(2,1)S(1)}, bf16[256,1024]{1,0:T(8,128)(2,1)}, u32[]{:S(2)}) copy-start(bf16[256,1024]{1,0:T(8,128)(2,1)} %q.5) | copy-start | bytes 1572868
  3.1 2.1 %collective-permute-start = (f32[1024,128]{1,0:T(8,128)S(1)}, f32[1024,128]{1,0:T(8,128)S(1)}, u32[]{:S(2)}, u32[]{:S(2)}) collective-permute-start(f32[1024,128]{1,0:T(8,128)S(1)} %shard_map.93), channel_id=1, source_target_pairs={{0,4},{4,0},{8,12},{12,8},{16,20},{20,16},{24,28},{28,24},{1,5},{5... | collective-permute-start | bytes 1572872 | tf_op jit(solution)/shard_map/ppermute | solution.py:156
  5.2 9.5 %collective-permute-start.1 = (bf16[1024,128]{1,0:T(8,128)(2,1)S(1)}, bf16[1024,128]{1,0:T(8,128)(2,1)S(1)}, u32[]{:S(2)}, u32[]{:S(2)}) collective-permute-start(bf16[1024,128]{1,0:T(8,128)(2,1)S(1)} %get-tuple-element.37), channel_id=1, source_target_pairs={{0,8},{4,12},{8,0},{12,4},{16,24},{20,28},{24,16},{28,20},{1,9},{5... | collective-permute-start | bytes 786440 | tf_op jit(solution)/shard_map/ppermute | solution.py:156
  14.8 12.3 %collective-permute-start.2 = (bf16[1024,128]{1,0:T(8,128)(2,1)S(1)}, bf16[1024,128]{1,0:T(8,128)(2,1)}, u32[]{:S(2)}, u32[]{:S(2)}) collective-permute-start(bf16[1024,128]{1,0:T(8,128)(2,1)S(1)} %fusion.2), channel_id=1, source_target_pairs={{0,16},{4,20},{8,24},{12,28},{16,0},{20,4},{24,8},{28,12},{1,17},{... | collective-permute-start | bytes 786440 | tf_op jit(solution)/shard_map/ppermute | solution.py:156
  16.7 37.6 %collective-permute-start.9 = (bf16[256,1024]{1,0:T(8,128)(2,1)}, bf16[256,1024]{1,0:T(8,128)(2,1)S(1)}, u32[]{:S(2)}, u32[]{:S(2)}) collective-permute-start(bf16[256,1024]{1,0:T(8,128)(2,1)} %refs_0_.5), channel_id=1, source_target_pairs={{0,2},{1,3},{2,0},{3,1},{4,6},{5,7},{6,4},{7,5},{8,10},{9,11},{10,... | collective-permute-start | bytes 1572872 | tf_op jit(solution)/shard_map/ppermute | solution.py:184
  19.2 35.0 %collective-permute-start.10 = (bf16[256,1024]{1,0:T(8,128)(2,1)}, bf16[256,1024]{1,0:T(8,128)(2,1)}, u32[]{:S(2)}, u32[]{:S(2)}) collective-permute-start(bf16[256,1024]{1,0:T(8,128)(2,1)} %refs_0_.5), channel_id=1, source_target_pairs={{0,1},{1,2},{2,3},{3,0},{4,5},{5,6},{6,7},{7,4},{8,9},{9,10},{10,1... | collective-permute-start | bytes 1572872 | tf_op jit(solution)/shard_map/ppermute | solution.py:184
  20.8 33.9 %collective-permute-start.11 = (bf16[256,1024]{1,0:T(8,128)(2,1)}, bf16[256,1024]{1,0:T(8,128)(2,1)}, u32[]{:S(2)}, u32[]{:S(2)}) collective-permute-start(bf16[256,1024]{1,0:T(8,128)(2,1)} %refs_0_.5), channel_id=1, source_target_pairs={{0,3},{1,0},{2,1},{3,2},{4,7},{5,4},{6,5},{7,6},{8,11},{9,8},{10,9... | collective-permute-start | bytes 1572872 | tf_op jit(solution)/shard_map/ppermute | solution.py:184
  32.2 22.6 %copy-start.11 = (bf16[256,1024]{1,0:T(8,128)(2,1)S(1)}, bf16[256,1024]{1,0:T(8,128)(2,1)}, u32[]{:S(2)}) copy-start(bf16[256,1024]{1,0:T(8,128)(2,1)} %refs_0_.5) | copy-start | bytes 1572868
  34.2 22.0 %copy-start.25 = (f32[256,1024]{1,0:T(8,128)}, f32[256,1024]{1,0:T(8,128)S(1)}, u32[]{:S(2)}) copy-start(f32[256,1024]{1,0:T(8,128)S(1)} %get-tuple-element.25) | copy-start | bytes 3145732
  34.3 23.5 %copy-start.23 = (f32[256,1024]{1,0:T(8,128)}, f32[256,1024]{1,0:T(8,128)S(1)}, u32[]{:S(2)}) copy-start(f32[256,1024]{1,0:T(8,128)S(1)} %get-tuple-element.22) | copy-start | bytes 3145732
  34.3 36.3 %collective-permute-start.3 = (bf16[256,1024]{1,0:T(8,128)(2,1)S(1)}, bf16[256,1024]{1,0:T(8,128)(2,1)S(1)}, u32[]{:S(2)}, u32[]{:S(2)}) collective-permute-start(bf16[256,1024]{1,0:T(8,128)(2,1)S(1)} %get-tuple-element.24), channel_id=1, source_target_pairs={{0,1},{4,5},{8,9},{12,13},{16,17},{20,21},{24,25},{28,29}} | collective-permute-start | bytes 1572872 | tf_op jit(solution)/shard_map/ppermute | solution.py:234
  36.0 36.2 %collective-permute-start.6 = (bf16[256,1024]{1,0:T(8,128)(2,1)S(1)}, bf16[256,1024]{1,0:T(8,128)(2,1)S(1)}, u32[]{:S(2)}, u32[]{:S(2)}) collective-permute-start(bf16[256,1024]{1,0:T(8,128)(2,1)S(1)} %get-tuple-element.26), channel_id=1, source_target_pairs={{3,2},{7,6},{11,10},{15,14},{19,18},{23,22},{27,26},{31,30}} | collective-permute-start | bytes 1572872 | tf_op jit(solution)/shard_map/ppermute | solution.py:237
  56.2 18.7 %collective-permute-start.18 = (bf16[256,1024]{1,0:T(8,128)(2,1)S(1)}, bf16[256,1024]{1,0:T(8,128)(2,1)S(1)}, u32[]{:S(2)}, u32[]{:S(2)}) collective-permute-start(bf16[256,1024]{1,0:T(8,128)(2,1)S(1)} %get-tuple-element.41), channel_id=1, source_target_pairs={{0,8},{4,12},{8,0},{12,4},{16,24},{20,28},{24,16},{28,20},{1,9},{5... | collective-permute-start | bytes 1572872 | tf_op jit(solution)/shard_map/ppermute | solution.py:312
  57.8 18.5 %collective-permute-start.19 = (bf16[256,1024]{1,0:T(8,128)(2,1)S(1)}, bf16[256,1024]{1,0:T(8,128)(2,1)S(1)}, u32[]{:S(2)}, u32[]{:S(2)}) collective-permute-start(bf16[256,1024]{1,0:T(8,128)(2,1)S(1)} %get-tuple-element.40), channel_id=1, source_target_pairs={{0,16},{4,20},{8,24},{12,28},{16,0},{20,4},{24,8},{28,12},{1,17},{... | collective-permute-start | bytes 1572872 | tf_op jit(solution)/shard_map/ppermute | solution.py:312
  68.6 10.0 %collective-permute-start.12 = (f32[1024,128]{1,0:T(8,128)S(1)}, f32[1024,128]{1,0:T(8,128)S(1)}, u32[]{:S(2)}, u32[]{:S(2)}) collective-permute-start(f32[1024,128]{1,0:T(8,128)S(1)} %get-tuple-element.32), channel_id=1, source_target_pairs={{0,4},{4,0},{8,12},{12,8},{16,20},{20,16},{24,28},{28,24},{1,5},{5... | collective-permute-start | bytes 1572872 | tf_op jit(solution)/shard_map/ppermute | solution.py:156
  70.6 15.9 %copy-start.21 = (f32[256,1024]{1,0:T(8,128)}, f32[256,1024]{1,0:T(8,128)S(1)}, u32[]{:S(2)}) copy-start(f32[256,1024]{1,0:T(8,128)S(1)} %get-tuple-element.21) | copy-start | bytes 3145732
  70.6 66.6 %copy-start.5 = (bf16[256,1024]{1,0:T(8,128)(2,1)S(1)}, bf16[256,1024]{1,0:T(8,128)(2,1)}, u32[]{:S(2)}) copy-start(bf16[256,1024]{1,0:T(8,128)(2,1)} %k.7) | copy-start | bytes 1572868
  70.6 66.6 %copy-start.8 = (bf16[256,1024]{1,0:T(8,128)(2,1)S(1)}, bf16[256,1024]{1,0:T(8,128)(2,1)}, u32[]{:S(2)}) copy-start(bf16[256,1024]{1,0:T(8,128)(2,1)} %v.7) | copy-start | bytes 1572868
  70.6 15.8 %collective-permute-start.20 = (bf16[256,1024]{1,0:T(8,128)(2,1)S(1)}, bf16[256,1024]{1,0:T(8,128)(2,1)S(1)}, u32[]{:S(2)}, u32[]{:S(2)}) collective-permute-start(bf16[256,1024]{1,0:T(8,128)(2,1)S(1)} %get-tuple-element.39), channel_id=1, source_target_pairs={{0,24},{4,28},{8,16},{12,20},{16,8},{20,12},{24,0},{28,4},{1,25},{... | collective-permute-start | bytes 1572872 | tf_op jit(solution)/shard_map/ppermute | solution.py:312
  72.2 25.6 %collective-permute-start.15 = (bf16[256,1024]{1,0:T(8,128)(2,1)S(1)}, bf16[256,1024]{1,0:T(8,128)(2,1)}, u32[]{:S(2)}, u32[]{:S(2)}) collective-permute-start(bf16[256,1024]{1,0:T(8,128)(2,1)S(1)} %get-tuple-element.20.normed.refs_0_), channel_id=1, source_target_pairs={{0,8},{4,12},{8,0},{12,4},{16,24},{20,28},{24,16},{28,20},{1,9},{5... | collective-permute-start | bytes 1572872 | tf_op jit(solution)/shard_map/ppermute | solution.py:244
  75.8 34.3 %collective-permute-start.16 = (bf16[256,1024]{1,0:T(8,128)(2,1)S(1)}, bf16[256,1024]{1,0:T(8,128)(2,1)}, u32[]{:S(2)}, u32[]{:S(2)}) collective-permute-start(bf16[256,1024]{1,0:T(8,128)(2,1)S(1)} %get-tuple-element.20.normed.refs_0_), channel_id=1, source_target_pairs={{0,16},{4,20},{8,24},{12,28},{16,0},{20,4},{24,8},{28,12},{1,17},{... | collective-permute-start | bytes 1572872 | tf_op jit(solution)/shard_map/ppermute | solution.py:244
  77.1 33.0 %collective-permute-start.17 = (bf16[256,1024]{1,0:T(8,128)(2,1)S(1)}, bf16[256,1024]{1,0:T(8,128)(2,1)}, u32[]{:S(2)}, u32[]{:S(2)}) collective-permute-start(bf16[256,1024]{1,0:T(8,128)(2,1)S(1)} %get-tuple-element.20.normed.refs_0_), channel_id=1, source_target_pairs={{0,24},{4,28},{8,16},{12,20},{16,8},{20,12},{24,0},{28,4},{1,25},{... | collective-permute-start | bytes 1572872 | tf_op jit(solution)/shard_map/ppermute | solution.py:244
  78.6 8.7 %copy-start.28 = (f32[1024,128]{1,0:T(8,128)}, f32[1024,128]{1,0:T(8,128)S(1)}, u32[]{:S(2)}) copy-start(f32[1024,128]{1,0:T(8,128)S(1)} %collective-permute-done.12) | copy-start | bytes 1572868
  78.6 40.5 %collective-permute-start.7 = (bf16[256,1024]{1,0:T(8,128)(2,1)}, bf16[256,1024]{1,0:T(8,128)(2,1)}, u32[]{:S(2)}, u32[]{:S(2)}) collective-permute-start(bf16[256,1024]{1,0:T(8,128)(2,1)} %get-tuple-element.44), channel_id=1, source_target_pairs={{2,1},{3,2},{6,5},{7,6},{10,9},{11,10},{14,13},{15,14},{18,17},{19... | collective-permute-start | bytes 1572872 | tf_op jit(solution)/shard_map/ppermute | solution.py:237
  87.2 29.5 %collective-permute-start.13 = (bf16[1024,128]{1,0:T(8,128)(2,1)}, bf16[1024,128]{1,0:T(8,128)(2,1)S(1)}, u32[]{:S(2)}, u32[]{:S(2)}) collective-permute-start(bf16[1024,128]{1,0:T(8,128)(2,1)} %get-tuple-element.35), channel_id=1, source_target_pairs={{0,8},{4,12},{8,0},{12,4},{16,24},{20,28},{24,16},{28,20},{1,9},{5... | collective-permute-start | bytes 786440 | tf_op jit(solution)/shard_map/ppermute | solution.py:156
  97.8 24.9 %collective-permute-start.4 = (bf16[256,1024]{1,0:T(8,128)(2,1)}, bf16[256,1024]{1,0:T(8,128)(2,1)S(1)}, u32[]{:S(2)}, u32[]{:S(2)}) collective-permute-start(bf16[256,1024]{1,0:T(8,128)(2,1)} %get-tuple-element.43), channel_id=1, source_target_pairs={{0,1},{1,2},{4,5},{5,6},{8,9},{9,10},{12,13},{13,14},{16,17},{17,1... | collective-permute-start | bytes 1572872 | tf_op jit(solution)/shard_map/ppermute | solution.py:234
  113.2 9.5 %copy-start.24 = (f32[256,1024]{1,0:T(8,128)S(1)}, f32[256,1024]{1,0:T(8,128)}, u32[]{:S(2)}) copy-start(f32[256,1024]{1,0:T(8,128)} %copy-done.23) | copy-start | bytes 3145732
  116.7 28.0 %collective-permute-start.21 = (bf16[1024,512]{1,0:T(8,128)(2,1)}, bf16[1024,512]{1,0:T(8,128)(2,1)}, u32[]{:S(2)}, u32[]{:S(2)}) collective-permute-start(bf16[1024,512]{1,0:T(8,128)(2,1)} %shard_map.101), channel_id=1, source_target_pairs={{0,4},{4,0},{8,12},{12,8},{16,20},{20,16},{24,28},{28,24},{1,5},{5... | collective-permute-start | bytes 3145736 | tf_op jit(solution)/shard_map/ppermute | solution.py:345
  118.6 23.3 %collective-permute-start.14 = (bf16[1024,128]{1,0:T(8,128)(2,1)}, bf16[1024,128]{1,0:T(8,128)(2,1)}, u32[]{:S(2)}, u32[]{:S(2)}) collective-permute-start(bf16[1024,128]{1,0:T(8,128)(2,1)} %fusion.5), channel_id=1, source_target_pairs={{0,16},{4,20},{8,24},{12,28},{16,0},{20,4},{24,8},{28,12},{1,17},{... | collective-permute-start | bytes 786440 | tf_op jit(solution)/shard_map/ppermute | solution.py:156
  121.4 30.3 %collective-permute-start.8 = (bf16[256,1024]{1,0:T(8,128)(2,1)}, bf16[256,1024]{1,0:T(8,128)(2,1)}, u32[]{:S(2)}, u32[]{:S(2)}) collective-permute-start(bf16[256,1024]{1,0:T(8,128)(2,1)} %add_convert_fusion.1), channel_id=1, source_target_pairs={{1,0},{2,1},{3,2},{5,4},{6,5},{7,6},{9,8},{10,9},{11,10},{13,12},{... | collective-permute-start | bytes 1572872 | tf_op jit(solution)/shard_map/ppermute | solution.py:237
  123.7 28.1 %collective-permute-start.5 = (bf16[256,1024]{1,0:T(8,128)(2,1)}, bf16[256,1024]{1,0:T(8,128)(2,1)}, u32[]{:S(2)}, u32[]{:S(2)}) collective-permute-start(bf16[256,1024]{1,0:T(8,128)(2,1)} %add_convert_fusion.3), channel_id=1, source_target_pairs={{0,1},{1,2},{2,3},{4,5},{5,6},{6,7},{8,9},{9,10},{10,11},{12,13},{... | collective-permute-start | bytes 1572872 | tf_op jit(solution)/shard_map/ppermute | solution.py:234
  137.2 14.5 %copy-start.22 = (f32[256,1024]{1,0:T(8,128)S(1)}, f32[256,1024]{1,0:T(8,128)}, u32[]{:S(2)}) copy-start(f32[256,1024]{1,0:T(8,128)} %copy-done.21) | copy-start | bytes 3145732
  (19 other events, 26.3 us)
where the time goes:
time: 155 us; the launch traced here: 154 us
  starting transfers between devices  50.9 us (33%)
  waiting for transfers between devices  41.6 us (27%)
  Pallas kernels  24.4 us (16%)
  local copies, waits for them, and re-layouts  22.6 us (15%)
  other arithmetic  13.4 us (9%)
    ppermute x3, starting transfers between devices, body(): lax.ppermute(send_right, 'head', [(i, i + 1) for i in range(min(r, n_head...  27.5 us
    pallas_call x11, Pallas kernels, kernel_call(): pl.pallas_call(kernel, compiler_params=pltpu.CompilerParams(vmem_limit_by...  24.4 us
    unnamed x58, local copies, waits for them, and re-layouts  22.6 us
    ppermute x3, waiting for transfers between devices, body(): slots.append(lax.ppermute(cotangent, 'head', shifted(n_head, r)))  18.1 us
    ppermute x3, waiting for transfers between devices, body(): rows.append(lax.ppermute(normed, 'ctx', perm))  10 us
    ppermute x6, waiting for transfers between devices, exclusive_sum(): other = lax.ppermute(sent, 'ctx', flipped(size, mask))  8.15 us
    ppermute x3, starting transfers between devices, body(): slots.append(lax.ppermute(cotangent, 'head', shifted(n_head, r)))  6.41 us
    ppermute x6, starting transfers between devices, exclusive_sum(): other = lax.ppermute(sent, 'ctx', flipped(size, mask))  6.39 us
  transfers between devices with their start and end apart: 22, of which 6 were waited for; matrix products, arithmetic and copies ran while one was open for 7% of the time, Pallas kernels for 16%

commit v1 on v0

v1 whole, which is shorter than its diff:
```python
import functools

import jax
import jax.numpy as jnp
from jax import lax
from jax.experimental import pallas as pl
from jax.experimental.pallas import tpu as pltpu
from jax.sharding import PartitionSpec as P


HEAD_DIM = 128

epsilon = 1e-06


bf16 = jnp.bfloat16
f32 = jnp.float32
VMEM = pl.BlockSpec(memory_space=pltpu.VMEM)
GRANT = 12 << 20


def mm(a, b, da, db):
    return lax.dot_general(a, b, (((da,), (db,)), ((), ())), preferred_element_type=f32)


def split(x):
    high = x.astype(bf16)
    return high, (x - high.astype(f32)).astype(bf16)


def head(h):
    return slice(h * HEAD_DIM, (h + 1) * HEAD_DIM)


def below(n):
    return lax.broadcasted_iota(jnp.int32, (n, n), 0) >= lax.broadcasted_iota(jnp.int32, (n, n), 1)


def array(shape, dtype):
    return jax.ShapeDtypeStruct(shape, dtype)


def kernel_call(kernel, *args, **settings):
    return pl.pallas_call(kernel, compiler_params=pltpu.CompilerParams(vmem_limit_bytes=GRANT), **settings)(*args)


def call(kernel, outs, *args):
    return kernel_call(
        kernel, *args, out_shape=outs, in_specs=[VMEM] * len(args), out_specs=jax.tree.map(lambda _: VMEM, outs)
    )


def state_kernel(k, v, out):
    for h in range(k.shape[1] // HEAD_DIM):
        out[head(h), :] = mm(k[:, head(h)], v[:, head(h)], 0, 0)


def intra_kernel(q, k, v, out):
    keep = below(q.shape[0])
    for h in range(q.shape[1] // HEAD_DIM):
        scores = jnp.where(keep, mm(q[:, head(h)], k[:, head(h)], 1, 1), 0.0).astype(bf16)
        out[:, head(h)] = mm(scores, v[:, head(h)], 1, 0)


def step_kernel(mask, upward, fresh, last, at, total, *refs):
    outer, other, outs = None if fresh else refs[0], refs[0 if fresh else 1], refs[1 if fresh else 2 :]
    value = other[...].astype(f32)
    outs[0][...] = jnp.zeros_like(value) if fresh else outer[...]
    upper = lax.rem(lax.div(at[1], mask), 2)

    @pl.when(upper == (1 if upward else 0))
    def _():
        outs[0][...] += value

    if not last:
        whole = total[...] + value
        outs[1][...] = whole
        outs[2][...] = whole.astype(bf16)


def row_scale_of(attended):
    return lax.rsqrt(jnp.mean(attended * attended, axis=-1, keepdims=True) + epsilon)


def norm_kernel(q, intra, prefix, attended, normed):
    for h in range(q.shape[1] // HEAD_DIM):
        high, low = split(prefix[head(h), :])
        query = q[:, head(h)]
        value = intra[:, head(h)] + mm(query, high, 1, 0) + mm(query, low, 1, 0)
        attended[:, head(h)] = value
        normed[:, head(h)] = (value * row_scale_of(value)).astype(bf16)


def block_at(ref, block, width):
    return ref[:, pl.ds(pl.multiple_of(block * width, width), width)]


def piece_kernel(block_of, at, weight, normed, *refs):
    extras, out = refs[:-1], refs[-1]
    value = mm(normed[...], block_at(weight, block_of(at[0]), out.shape[1]), 1, 0)
    for ref in extras:
        value = value + ref[...].astype(f32)
    out[...] = value.astype(bf16)


def add_terms(out, place, blocks, sources, weight):
    for ref, source in zip(blocks, sources):
        block, valid = source(place)

        @pl.when(valid)
        def _(ref=ref, block=block):
            out[...] += mm(ref[...], block_at(weight, block, ref.shape[1]), 1, 1)


def upstream_kernel(own, sources, at, weight, first, *refs):
    blocks, out = refs[:-1], refs[-1]
    if own:
        out[...] = mm(first[...], block_at(weight, at[0], first.shape[1]), 1, 1)
    else:
        out[...] = first[...]
    add_terms(out, at[0], blocks, sources, weight)


def finish_kernel(sources, at, weight, so_far, attended, q, *refs):
    blocks, (d_out, grad_out, upstream) = refs[:-3], refs[-3:]
    upstream[...] = so_far[...]
    add_terms(upstream, at[0], blocks, sources, weight)
    for h in range(d_out.shape[1] // HEAD_DIM):
        value, up = attended[:, head(h)], upstream[:, head(h)]
        scale = row_scale_of(value)
        unit = value * scale
        grad = scale * (up - unit * jnp.mean(up * unit, axis=-1, keepdims=True))
        grad = grad.astype(bf16)
        d_out[:, head(h)] = grad
        grad_out[head(h), :] = mm(q[:, head(h)], grad, 0, 0)


def pick_kernel(choices, at, *refs):
    sources, outs = refs[: len(refs) - len(choices)], refs[len(refs) - len(choices) :]
    for choice, out in zip(choices, outs):
        chosen = choice(at[0], at[1])
        for m, source in enumerate(sources):

            @pl.when(chosen == m)
            def _(out=out, source=source):
                out[...] = source[...]


def back_kernel(q, k, v, d, prefix, grad_q, part_k, part_v):
    keep = below(q.shape[0])
    for h in range(q.shape[1] // HEAD_DIM):
        qh, kh, vh, dh = q[:, head(h)], k[:, head(h)], v[:, head(h)], d[:, head(h)]
        high, low = split(prefix[head(h), :])
        scores = jnp.where(keep, mm(qh, kh, 1, 1), 0.0).astype(bf16)
        back = jnp.where(keep, mm(dh, vh, 1, 1), 0.0).astype(bf16)
        grad_q[:, head(h)] = (mm(back, kh, 1, 0) + mm(dh, high, 1, 1) + mm(dh, low, 1, 1)).astype(bf16)
        part_k[:, head(h)] = mm(back, qh, 0, 0)
        part_v[:, head(h)] = mm(scores, dh, 0, 0)


def suffix_kernel(k, v, part_k, part_v, suffix, grad_k, grad_v):
    for h in range(k.shape[1] // HEAD_DIM):
        high, low = split(suffix[head(h), :])
        kh, vh = k[:, head(h)], v[:, head(h)]
        grad_k[:, head(h)] = (part_k[:, head(h)] + mm(vh, high, 1, 1) + mm(vh, low, 1, 1)).astype(bf16)
        grad_v[:, head(h)] = (part_v[:, head(h)] + mm(kh, high, 1, 0) + mm(kh, low, 1, 0)).astype(bf16)


def weight_grad_kernel(count, core_of, at, *refs):
    rows, cols = refs[:count], refs[count : 2 * count]
    out = refs[-1]
    own_cols = out.shape[1]
    value = None
    for n in range(count):
        term = mm(rows[n][...], block_at(cols[n], core_of(at[1]), own_cols), 0, 0)
        value = term if value is None else value + term
    for ref in refs[2 * count : -1]:
        value = value + ref[...].astype(f32)
    out[...] = value.astype(out.dtype)


def flipped(size, mask):
    return [(i, i ^ mask) for i in range(size)]


def make_body(n_ctx, n_head):
    pair = min(2, n_ctx)
    chips = n_ctx // pair

    def body(queries, key_rows, value_rows, out_weight, cotangent):
        length, width = queries.shape
        model = out_weight.shape[1]
        part = model // n_head
        chip_cols = model // chips
        own_cols = chip_cols // pair
        position = lax.axis_index("ctx")
        place = lax.axis_index("head")
        wide = array((length, width), f32)
        narrow = array((length, width), bf16)
        piece = array((length, part), bf16)

        where = jnp.where(jnp.arange(2) == 0, place, position).astype(jnp.int32)

        def placed(kernel, outs, *args, scratch=()):
            return kernel_call(
                kernel,
                where,
                *args,
                out_shape=outs,
                in_specs=[pl.BlockSpec(memory_space=pltpu.SMEM)] + [VMEM] * len(args),
                out_specs=jax.tree.map(lambda _: VMEM, outs),
                scratch_shapes=scratch,
            )

        def exclusive_sum(block, upward):
            total, sent, outer, mask = block, block, [], 1
            state, state_sent = array(block.shape, f32), array(block.shape, bf16)
            while mask < n_ctx:
                other = lax.ppermute(sent, "ctx", flipped(n_ctx, mask))
                last = 2 * mask >= n_ctx
                got = placed(
                    functools.partial(step_kernel, mask, upward, not outer, last),
                    [state] if last else [state, state, state_sent],
                    total,
                    *outer,
                    other,
                )
                outer = [got[0]]
                if not last:
                    _, total, sent = got
                mask *= 2
            return outer[0] if outer else jnp.zeros_like(block)

        def line(r, p):
            over = []
            for link in range(p, n_head - 1, 2):
                if link - r + 1 >= 0:
                    over.append((link, link + 1))
                if link + r < n_head:
                    over.append((link + 1, link))
            return over

        def block_of(r, p, place):
            block = jnp.where(lax.rem(place, 2) == p, place + r, place - r)
            valid = (block >= 0) & (block < n_head)
            return jnp.minimum(jnp.maximum(block, 0), n_head - 1), valid

        rounds = [(r, p) for r in range(1, n_head) for p in range(2) if line(r, p)]
        got = {(0, 0): cotangent, (0, 1): cotangent}
        for r, p in rounds:
            if r < n_head - 1 or r == 1:
                got[r, p] = lax.ppermute(got[r - 1, 1 - p], "head", line(r, p))

        block_state = call(state_kernel, array((width, HEAD_DIM), f32), key_rows, value_rows)
        intra = call(intra_kernel, wide, queries, key_rows, value_rows)
        prefix = exclusive_sum(block_state, True)
        attended, normed = call(norm_kernel, (wide, narrow), queries, intra, prefix)

        def piece_of(block, *extras):
            kernel = functools.partial(piece_kernel, block)
            return placed(kernel, piece, out_weight, normed, *extras)

        came = {}
        for r, p in sorted(rounds, key=lambda at: -at[0]):
            extras = [came[r + 1, 1 - p]] if (r + 1, 1 - p) in came else []
            sent = piece_of(lambda i, r=r, p=p: block_of(r, p, i)[0], *extras)
            back = [(j, i) for i, j in line(r, p)]
            if (r, p) in got:
                came[r, p] = lax.ppermute(sent, "head", back)
            else:
                ends = [i for i, _ in back]

                def gives(place, position, ends=ends):
                    return functools.reduce(jnp.logical_or, [place == i for i in ends]).astype(jnp.int32)

                (sent,) = placed(functools.partial(pick_kernel, [gives]), [piece], got[r - 1, 1 - p], sent)
                got[r, p] = came[r, p] = lax.ppermute(sent, "head", line(r, p) + back)
        mixed = piece_of(lambda i: i, *[came[at] for at in ((1, 0), (1, 1)) if at in came])

        masks = list(range(pair, n_ctx, pair))
        rows_by = {0: normed}
        for mask in masks:
            low = mask & -mask
            high = mask ^ low
            if high == 0 or pair == 1:
                sent, via = normed, flipped(n_ctx, mask)
            else:
                (sent,) = placed(
                    functools.partial(pick_kernel, [lambda place, position: lax.rem(position, pair)]),
                    [narrow],
                    rows_by[high],
                    rows_by[low],
                )
                via = [(i, i ^ (low if i % pair == 0 else high)) for i in range(n_ctx)]
            rows_by[mask] = lax.ppermute(sent, "ctx", via)
        rows = [rows_by[mask] for mask in [0] + masks]

        def sources_of(here):
            return [functools.partial(block_of, *at) for at in here]

        upstream = cotangent
        for r in range(1, max(2, n_head - 1)):
            here = [at for at in rounds if at[0] == r and r < n_head - 1]
            upstream = placed(
                functools.partial(upstream_kernel, r == 1, sources_of(here)),
                wide,
                out_weight,
                upstream,
                *[got[at] for at in here],
            )
        here = [at for at in rounds if at[0] == n_head - 1]
        d_attended, grad_block = placed(
            functools.partial(finish_kernel, sources_of(here)),
            (narrow, array((width, HEAD_DIM), f32)),
            out_weight,
            upstream,
            attended,
            queries,
            *[got[at] for at in here],
            scratch=[pltpu.VMEM((length, width), f32)],
        )

        if chip_cols == part:

            def choice_of(mask, place, position):
                target = lax.div(position ^ mask, pair)
                chosen = jnp.int32(0)
                for n, at in enumerate(rounds):
                    block, valid = block_of(*at, place)
                    chosen = jnp.where(valid & (block == target), n + 1, chosen)
                return chosen

            cols = placed(
                functools.partial(pick_kernel, [functools.partial(choice_of, mask) for mask in [0] + masks]),
                [piece] * chips,
                cotangent,
                *[got[at] for at in rounds],
            )
        else:
            whole = jnp.zeros((n_head, length, part), bf16)
            whole = lax.dynamic_update_index_in_dim(whole, cotangent, place, 0)
            for at in rounds:
                block, valid = block_of(*at, place)
                old = lax.dynamic_index_in_dim(whole, block, 0, keepdims=False)
                whole = lax.dynamic_update_index_in_dim(whole, jnp.where(valid, got[at], old), block, 0)
            whole = whole.transpose(1, 0, 2).reshape(length, model)
            starts = [lax.div(position ^ mask, pair) * chip_cols for mask in [0] + masks]
            cols = [lax.dynamic_slice(whole, (0, start), (length, chip_cols)) for start in starts]
        cols = list(cols)
        for n, mask in enumerate(masks):
            cols[n + 1] = lax.ppermute(cols[n + 1], "ctx", flipped(n_ctx, mask))

        grad_q, part_k, part_v = call(
            back_kernel, (narrow, wide, wide), queries, key_rows, value_rows, d_attended, prefix
        )
        suffix = exclusive_sum(grad_block, False)
        grad_k, grad_v = call(suffix_kernel, (narrow, narrow), key_rows, value_rows, part_k, part_v, suffix)

        def weight_grad(core_of, dtype, span, *extra):
            return placed(
                functools.partial(weight_grad_kernel, len(rows[span]), core_of),
                array((width, own_cols), dtype),
                *rows[span],
                *cols[span],
                *extra,
            )

        def same(position):
            return lax.rem(position, pair)

        def partner(position):
            return 1 - lax.rem(position, pair)

        most, last = slice(0, max(1, chips - 1)), slice(max(1, chips - 1), chips)
        extra = []
        if pair > 1:
            if chips > 1:
                part_other = weight_grad(partner, f32, most)
                other = weight_grad(partner, bf16, last, part_other)
            else:
                other = weight_grad(partner, bf16, most)
            extra = [lax.ppermute(other, "ctx", flipped(n_ctx, 1))]
        if chips > 1:
            part_own = weight_grad(same, f32, most)
            grad_out_weight = weight_grad(same, f32, last, part_own, *extra)
        else:
            grad_out_weight = weight_grad(same, f32, most, *extra)
        return mixed, grad_q, grad_k, grad_v, grad_out_weight

    return body


def solution(mesh):
    n_ctx, n_head = mesh.shape["ctx"], mesh.shape["head"]
    body = make_body(n_ctx, n_head)

    return jax.shard_map(
        body,
        mesh=mesh,
        in_specs=(P("ctx", "head"),) * 3 + (P("head", None), P("ctx", "head")),
        out_specs=(P("ctx", "head"),) * 4 + (P("head", "ctx"),),
        check_vma=False,
    )
```

time: 155 us -> 109 us (0.70)
  local copies, waits for them, and re-layouts: 22.6 us -> 2.09 us
  starting transfers between devices: 50.9 us -> 35.3 us
  other arithmetic: 13.4 us -> 0.01 us
  Pallas kernels: 24.4 us -> 34.6 us
  waiting for transfers between devices: 41.6 us -> 36.1 us
    unnamed x58 -> x14, local copies, waits for them, and re-layouts: 22.6 us -> 2.09 us
    ppermute x22, starting transfers between devices: 50.9 us -> 35.3 us  [the longest x4 8.37 us: body(): came[r, p] = lax.ppermute(sent, 'head', back)]
    pallas_call x11 -> x27, Pallas kernels: 24.4 us -> 34.6 us  [kernel_call(): pl.pallas_call(kernel, compiler_params=pltpu.CompilerParams(vmem_limit_by...]
    convert_element_type x8 -> x0, other arithmetic: 9.68 us -> none  [the longest x4 2.89 us: exclusive_sum(): sent = total if mask == 1 else total.astype(bf16)]
    ppermute x22, waiting for transfers between devices: 41.6 us -> 36.1 us  [the longest x3 10.8 us: body(): cols[n + 1] = lax.ppermute(cols[n + 1], 'ctx', flipped(n_ctx, mask))]
    add x2 -> x0, other arithmetic: 2.32 us -> none  [exclusive_sum(): outer = outer + jnp.where(take, other, 0.0)]
  transfers between devices with their start and end apart: 22 -> 22, of which waited for: 6 -> 8; matrix products, arithmetic and copies ran while one was open for 7% -> 0% of each run, Pallas kernels for 16% -> 29%
where the time goes in v1:
time: 109 us
  waiting for transfers between devices  36.1 us (33%)
  starting transfers between devices  35.3 us (32%)
  Pallas kernels  34.6 us (32%)
  local copies, waits for them, and re-layouts  2.09 us (2%)
    pallas_call x27, Pallas kernels, kernel_call(): pl.pallas_call(kernel, compiler_params=pltpu.CompilerParams(vmem_limit_by...  34.6 us
    ppermute x3, waiting for transfers between devices, body(): cols[n + 1] = lax.ppermute(cols[n + 1], 'ctx', flipped(n_ctx, mask))  10.8 us
    ppermute x1, waiting for transfers between devices, body(): got[r, p] = came[r, p] = lax.ppermute(sent, 'head', line(r, p) + back)  9.95 us
    ppermute x4, waiting for transfers between devices, body(): got[r, p] = lax.ppermute(got[r - 1, 1 - p], 'head', line(r, p))  8.92 us
    ppermute x4, starting transfers between devices, body(): came[r, p] = lax.ppermute(sent, 'head', back)  8.37 us
    ppermute x1, starting transfers between devices, body(): got[r, p] = came[r, p] = lax.ppermute(sent, 'head', line(r, p) + back)  7.09 us
    ppermute x6, starting transfers between devices, exclusive_sum(): other = lax.ppermute(sent, 'ctx', flipped(n_ctx, mask))  6.84 us
    ppermute x6, waiting for transfers between devices, exclusive_sum(): other = lax.ppermute(sent, 'ctx', flipped(n_ctx, mask))  5.36 us
  transfers between devices with their start and end apart: 22, of which 8 were waited for; matrix products, arithmetic and copies ran while one was open for 0% of the time, Pallas kernels for 29%

profile of v1, /device:TPU:0, one launch (start us, length us, event | category | flops | bytes accessed | tf_op | source)
XLA Modules:
  0.0 109.1 jit_solution(7388649235866672596)
XLA Ops:
  3.6 2.6 %collective-permute-start.3 = (bf16[256,1024]{1,0:T(8,128)(2,1)}, bf16[256,1024]{1,0:T(8,128)(2,1)S(1)}, u32[]{:S(2)}, u32[]{:S(2)}) collective-permute-start(bf16[256,1024]{1,0:T(8,128)(2,1)} %refs_0_.1), channel_id=1, source_target_pairs={{0,1},{1,0},{2,3},{3,2},{4,5},{5,4},{6,7},{7,6},{8,9},{9,8},{10,11... | collective-permute-start | bytes 1572872 | tf_op jit(solution)/shard_map/ppermute | solution.py:252
  6.3 1.3 %shard_map.94 = (f32[1024,128]{1,0:T(8,128)S(1)}, f32[1024,128]{1,0:T(8,128)S(1)}, bf16[1024,128]{1,0:T(8,128)(2,1)S(1)}) custom-call(s32[2]{0:T(128)S(1)} %compare_select_fusion.at, f32[1024,128]{1,0:T(8,128)S(1)} %shard_map.93.total, f32[1024,128]{1,0:T(8,128)} %collective-permute-done.refs_0_), custom_call_target="tpu_custom_call" | custom-call | tf_op jit(solution)/shard_map/pallas_call | solution.py:44
  7.6 1.9 %collective-permute-start.1 = (bf16[1024,128]{1,0:T(8,128)(2,1)S(1)}, bf16[1024,128]{1,0:T(8,128)(2,1)S(1)}, u32[]{:S(2)}, u32[]{:S(2)}) collective-permute-start(bf16[1024,128]{1,0:T(8,128)(2,1)S(1)} %get-tuple-element.32), channel_id=1, source_target_pairs={{0,8},{4,12},{8,0},{12,4},{16,24},{20,28},{24,16},{28,20},{1,9},{5... | collective-permute-start | bytes 786440 | tf_op jit(solution)/shard_map/ppermute | solution.py:219
  10.2 8.8 %collective-permute-done.3.refs_0_.refs_1_ = bf16[256,1024]{1,0:T(8,128)(2,1)S(1)} collective-permute-done((bf16[256,1024]{1,0:T(8,128)(2,1)}, bf16[256,1024]{1,0:T(8,128)(2,1)S(1)}, u32[]{:S(2)}, u32[]{:S(2)}) %collective-permute-start.3) | collective-permute-done | bytes 524320 | tf_op jit(solution)/shard_map/ppermute | solution.py:252
  20.4 1.7 %collective-permute-start.2 = (bf16[1024,128]{1,0:T(8,128)(2,1)S(1)}, bf16[1024,128]{1,0:T(8,128)(2,1)S(1)}, u32[]{:S(2)}, u32[]{:S(2)}) collective-permute-start(bf16[1024,128]{1,0:T(8,128)(2,1)S(1)} %get-tuple-element.35), channel_id=1, source_target_pairs={{0,16},{4,20},{8,24},{12,28},{16,0},{20,4},{24,8},{28,12},{1,17},{... | collective-permute-start | bytes 786440 | tf_op jit(solution)/shard_map/ppermute | solution.py:219
  23.1 1.3 %collective-permute-start.11 = (bf16[256,1024]{1,0:T(8,128)(2,1)S(1)}, bf16[256,1024]{1,0:T(8,128)(2,1)S(1)}, u32[]{:S(2)}, u32[]{:S(2)}) collective-permute-start(bf16[256,1024]{1,0:T(8,128)(2,1)S(1)} %collective-permute-done.10.refs_1_.refs_2_), channel_id=1, source_target_pairs={{1,0},{2,3},{5,4},{6,7},{9,8},{10,11},{13,12},{14,15},{17,16},{18,... | collective-permute-start | bytes 1572872 | tf_op jit(solution)/shard_map/ppermute | solution.py:252
  24.4 4.1 %collective-permute-done.2.refs_1_ = bf16[1024,128]{1,0:T(8,128)(2,1)S(1)} collective-permute-done((bf16[1024,128]{1,0:T(8,128)(2,1)S(1)}, bf16[1024,128]{1,0:T(8,128)(2,1)S(1)}, u32[]{:S(2)}, u32[]{:S(2)}) %collective-permute-start.2) | collective-permute-done | bytes 262176 | tf_op jit(solution)/shard_map/ppermute | solution.py:219
  29.7 1.3 %shard_map.98.refs_1_ = bf16[256,1024]{1,0:T(8,128)(2,1)S(1)} custom-call(s32[2]{0:T(128)S(1)} %compare_select_fusion.at, bf16[1024,4096]{1,0:T(8,128)(2,1)S(1)} %copy-done, bf16[256,1024]{1,0:T(8,128)(2,1)S(1)} %get-tuple-element.36.normed.refs_0_), custom_call_target="tpu_custom_call" | custom-call | tf_op jit(solution)/shard_map/pallas_call | solution.py:44
  31.5 7.1 %collective-permute-start.5 = (bf16[256,1024]{1,0:T(8,128)(2,1)S(1)}, bf16[256,1024]{1,0:T(8,128)(2,1)S(1)}, u32[]{:S(2)}, u32[]{:S(2)}) collective-permute-start(bf16[256,1024]{1,0:T(8,128)(2,1)S(1)} %shard_map.99), channel_id=1, source_target_pairs={{1,0},{2,3},{0,1},{3,2},{5,4},{6,7},{4,5},{7,6},{9,8},{10,11},{8,9... | collective-permute-start | bytes 1572872 | tf_op jit(solution)/shard_map/ppermute | solution.py:277
  39.4 1.5 %collective-permute-start.15 = (bf16[256,1024]{1,0:T(8,128)(2,1)S(1)}, bf16[256,1024]{1,0:T(8,128)(2,1)S(1)}, u32[]{:S(2)}, u32[]{:S(2)}) collective-permute-start(bf16[256,1024]{1,0:T(8,128)(2,1)S(1)} %get-tuple-element.36.normed.refs_0_), channel_id=1, source_target_pairs={{0,16},{4,20},{8,24},{12,28},{16,0},{20,4},{24,8},{28,12},{1,17},{... | collective-permute-start | bytes 1572872 | tf_op jit(solution)/shard_map/ppermute | solution.py:295
  41.1 10.0 %collective-permute-done.5.refs_0_.refs_5_ = bf16[256,1024]{1,0:T(8,128)(2,1)S(1)} collective-permute-done((bf16[256,1024]{1,0:T(8,128)(2,1)S(1)}, bf16[256,1024]{1,0:T(8,128)(2,1)S(1)}, u32[]{:S(2)}, u32[]{:S(2)}) %collective-permute-start.5) | collective-permute-done | bytes 524320 | tf_op jit(solution)/shard_map/ppermute | solution.py:277
  51.9 1.6 %collective-permute-start.19 = (bf16[256,1024]{1,0:T(8,128)(2,1)S(1)}, bf16[256,1024]{1,0:T(8,128)(2,1)S(1)}, u32[]{:S(2)}, u32[]{:S(2)}) collective-permute-start(bf16[256,1024]{1,0:T(8,128)(2,1)S(1)} %get-tuple-element.53), channel_id=1, source_target_pairs={{0,8},{4,12},{8,0},{12,4},{16,24},{20,28},{24,16},{28,20},{1,9},{5... | collective-permute-start | bytes 1572872 | tf_op jit(solution)/shard_map/ppermute | solution.py:351
  54.0 1.4 %collective-permute-start.18 = (bf16[256,1024]{1,0:T(8,128)(2,1)S(1)}, bf16[256,1024]{1,0:T(8,128)(2,1)S(1)}, u32[]{:S(2)}, u32[]{:S(2)}) collective-permute-start(bf16[256,1024]{1,0:T(8,128)(2,1)S(1)} %get-tuple-element.51), channel_id=1, source_target_pairs={{0,24},{4,28},{8,16},{12,20},{16,8},{20,12},{24,0},{28,4},{1,25},{... | collective-permute-start | bytes 1572872 | tf_op jit(solution)/shard_map/ppermute | solution.py:351
  56.1 1.6 %collective-permute-start.17 = (bf16[256,1024]{1,0:T(8,128)(2,1)S(1)}, bf16[256,1024]{1,0:T(8,128)(2,1)S(1)}, u32[]{:S(2)}, u32[]{:S(2)}) collective-permute-start(bf16[256,1024]{1,0:T(8,128)(2,1)S(1)} %shard_map.113), channel_id=1, source_target_pairs={{0,8},{4,20},{8,0},{12,28},{16,24},{20,4},{24,16},{28,12},{1,9},{5... | collective-permute-start | bytes 1572872 | tf_op jit(solution)/shard_map/ppermute | solution.py:295
  57.7 2.0 %shard_map.105.first = f32[256,1024]{1,0:T(8,128)S(1)} custom-call(s32[2]{0:T(128)S(1)} %compare_select_fusion.at, bf16[1024,4096]{1,0:T(8,128)(2,1)S(1)} %copy-done, bf16[256,1024]{1,0:T(8,128)(2,1)S(1)} %copy-done.6, bf16[256,1024]{1,0:T(8,128)(2,1)S(1)} %collective-permute-done.3.refs_0_.refs_1_, bf16[256,1024]{1,0:T(8,128)(2,1)S(1)} %collective-permute-done.10.refs_1_.refs_2_), custom_call_target="tpu_custom_call" | custom-call | tf_op jit(solution)/shard_map/pallas_call | solution.py:44
  59.7 1.4 %shard_map.106.so_far = f32[256,1024]{1,0:T(8,128)S(1)} custom-call(s32[2]{0:T(128)S(1)} %compare_select_fusion.at, bf16[1024,4096]{1,0:T(8,128)(2,1)S(1)} %copy-done, f32[256,1024]{1,0:T(8,128)S(1)} %shard_map.105.first, bf16[256,1024]{1,0:T(8,128)(2,1)S(1)} %collective-permute-done.11.refs_0_.refs_3_, ...), custom_call_target="tpu_custom_call" | custom-call | tf_op jit(solution)/shard_map/pallas_call | solution.py:44
  61.1 2.6 %shard_map.107 = (bf16[256,1024]{1,0:T(8,128)(2,1)S(1)}, f32[1024,128]{1,0:T(8,128)S(1)}) custom-call(s32[2]{0:T(128)S(1)} %compare_select_fusion.at, bf16[1024,4096]{1,0:T(8,128)(2,1)S(1)} %copy-done, f32[256,1024]{1,0:T(8,128)S(1)} %shard_map.106.so_far, f32[256,1024]{1,0:T(8,128)S(1)} %get-tuple-element.37.attended, bf16[256,1024]{1,0:T(8,128)(2,1)S(1)} %copy-done.5, ...), custom_call_target="tpu_custom_call" | custom-call | tf_op jit(solution)/shard_map/pallas_call | solution.py:44
  63.8 1.3 %shard_map.102 = bf16[256,1024]{1,0:T(8,128)(2,1)S(1)} custom-call(s32[2]{0:T(128)S(1)} %compare_select_fusion.at, bf16[1024,4096]{1,0:T(8,128)(2,1)S(1)} %copy-done, bf16[256,1024]{1,0:T(8,128)(2,1)S(1)} %get-tuple-element.36.normed.refs_0_), custom_call_target="tpu_custom_call" | custom-call | tf_op jit(solution)/shard_map/pallas_call | solution.py:44
  65.1 1.3 %shard_map.100 = bf16[256,1024]{1,0:T(8,128)(2,1)S(1)} custom-call(s32[2]{0:T(128)S(1)} %compare_select_fusion.at, bf16[1024,4096]{1,0:T(8,128)(2,1)S(1)} %copy-done, bf16[256,1024]{1,0:T(8,128)(2,1)S(1)} %get-tuple-element.36.normed.refs_0_, bf16[256,1024]{1,0:T(8,128)(2,1)S(1)} %collective-permute-done.5.refs_0_.refs_5_), custom_call_target="tpu_custom_call" | custom-call | tf_op jit(solution)/shard_map/pallas_call | solution.py:44
  66.8 2.4 %collective-permute-start.8 = (bf16[256,1024]{1,0:T(8,128)(2,1)S(1)}, bf16[256,1024]{1,0:T(8,128)(2,1)S(1)}, u32[]{:S(2)}, u32[]{:S(2)}) collective-permute-start(bf16[256,1024]{1,0:T(8,128)(2,1)S(1)} %shard_map.102), channel_id=1, source_target_pairs={{0,1},{3,2},{4,5},{7,6},{8,9},{11,10},{12,13},{15,14},{16,17},{19,... | collective-permute-start | bytes 1572872 | tf_op jit(solution)/shard_map/ppermute | solution.py:269
  69.2 10.4 %collective-permute-done.20.refs_5_ = bf16[256,1024]{1,0:T(8,128)(2,1)S(1)} collective-permute-done((bf16[256,1024]{1,0:T(8,128)(2,1)S(1)}, bf16[256,1024]{1,0:T(8,128)(2,1)S(1)}, u32[]{:S(2)}, u32[]{:S(2)}) %collective-permute-start.20) | collective-permute-done | bytes 524320 | tf_op jit(solution)/shard_map/ppermute | solution.py:351
  80.4 1.6 %shard_map.116.refs_2_ = f32[1024,512]{1,0:T(8,128)S(1)} custom-call(s32[2]{0:T(128)S(1)} %compare_select_fusion.at, bf16[256,1024]{1,0:T(8,128)(2,1)S(1)} %get-tuple-element.36.normed.refs_0_, bf16[256,1024]{1,0:T(8,128)(2,1)S(1)} %collective-permute-done.16.refs_1_, bf16[256,1024]{1,0:T(8,128)(2,1)S(1)} %collective-permute-done.15.refs_0_.refs_2_, ...), custom_call_target="tpu_custom_call" | custom-call | tf_op jit(solution)/shard_map/pallas_call | solution.py:44
  84.9 1.3 %shard_map.103 = bf16[256,1024]{1,0:T(8,128)(2,1)S(1)} custom-call(s32[2]{0:T(128)S(1)} %compare_select_fusion.at, bf16[1024,4096]{1,0:T(8,128)(2,1)S(1)} %copy-done, bf16[256,1024]{1,0:T(8,128)(2,1)S(1)} %get-tuple-element.36.normed.refs_0_, bf16[256,1024]{1,0:T(8,128)(2,1)S(1)} %collective-permute-done.8.refs_0_), custom_call_target="tpu_custom_call" | custom-call | tf_op jit(solution)/shard_map/pallas_call | solution.py:44
  86.9 1.3 %shard_map.101 = bf16[256,1024]{1,0:T(8,128)(2,1)S(1)} custom-call(s32[2]{0:T(128)S(1)} %compare_select_fusion.at, bf16[1024,4096]{1,0:T(8,128)(2,1)S(1)} %copy-done, bf16[256,1024]{1,0:T(8,128)(2,1)S(1)} %get-tuple-element.36.normed.refs_0_, bf16[256,1024]{1,0:T(8,128)(2,1)S(1)} %collective-permute-done.6.refs_0_), custom_call_target="tpu_custom_call" | custom-call | tf_op jit(solution)/shard_map/pallas_call | solution.py:44
  88.2 4.4 %collective-permute-start.7 = (bf16[256,1024]{1,0:T(8,128)(2,1)S(1)}, bf16[256,1024]{1,0:T(8,128)(2,1)S(1)}, u32[]{:S(2)}, u32[]{:S(2)}) collective-permute-start(bf16[256,1024]{1,0:T(8,128)(2,1)S(1)} %shard_map.101), channel_id=1, source_target_pairs={{1,0},{0,1},{3,2},{2,3},{5,4},{4,5},{7,6},{6,7},{9,8},{8,9},{11,10... | collective-permute-start | bytes 1572872 | tf_op jit(solution)/shard_map/ppermute | solution.py:269
  93.3 1.6 %collective-permute-start.14 = (bf16[1024,128]{1,0:T(8,128)(2,1)S(1)}, bf16[1024,128]{1,0:T(8,128)(2,1)S(1)}, u32[]{:S(2)}, u32[]{:S(2)}) collective-permute-start(bf16[1024,128]{1,0:T(8,128)(2,1)S(1)} %get-tuple-element.48), channel_id=1, source_target_pairs={{0,16},{4,20},{8,24},{12,28},{16,0},{20,4},{24,8},{28,12},{1,17},{... | collective-permute-start | bytes 786440 | tf_op jit(solution)/shard_map/ppermute | solution.py:219
  94.9 3.5 %shard_map.108 = (bf16[256,1024]{1,0:T(8,128)(2,1)}, f32[256,1024]{1,0:T(8,128)S(1)}, f32[256,1024]{1,0:T(8,128)S(1)}) custom-call(bf16[256,1024]{1,0:T(8,128)(2,1)S(1)} %copy-done.5, bf16[256,1024]{1,0:T(8,128)(2,1)S(1)} %copy-done.2, bf16[256,1024]{1,0:T(8,128)(2,1)S(1)} %copy-done.4, bf16[256,1024]{1,0:T(8,128)(2,1)S(1)} %get-tuple-element.38.d, ...), custom_call_target="tpu_custom_call" | custom-call | tf_op jit(solution)/shard_map/pallas_call | solution.py:44
  98.4 1.6 %shard_map.115.refs_2_ = f32[1024,512]{1,0:T(8,128)S(1)} custom-call(s32[2]{0:T(128)S(1)} %compare_select_fusion.at, bf16[256,1024]{1,0:T(8,128)(2,1)S(1)} %get-tuple-element.36.normed.refs_0_, bf16[256,1024]{1,0:T(8,128)(2,1)S(1)} %collective-permute-done.16.refs_1_, bf16[256,1024]{1,0:T(8,128)(2,1)S(1)} %collective-permute-done.15.refs_0_.refs_2_, ...), custom_call_target="tpu_custom_call" | custom-call | tf_op jit(solution)/shard_map/pallas_call | solution.py:44
  100.0 1.2 %collective-permute-done.14.refs_1_ = bf16[1024,128]{1,0:T(8,128)(2,1)S(1)} collective-permute-done((bf16[1024,128]{1,0:T(8,128)(2,1)S(1)}, bf16[1024,128]{1,0:T(8,128)(2,1)S(1)}, u32[]{:S(2)}, u32[]{:S(2)}) %collective-permute-start.14) | collective-permute-done | bytes 262176 | tf_op jit(solution)/shard_map/ppermute | solution.py:219
  101.9 1.7 %shard_map.112 = (bf16[256,1024]{1,0:T(8,128)(2,1)}, bf16[256,1024]{1,0:T(8,128)(2,1)}) custom-call(bf16[256,1024]{1,0:T(8,128)(2,1)S(1)} %copy-done.2, bf16[256,1024]{1,0:T(8,128)(2,1)S(1)} %copy-done.4, f32[256,1024]{1,0:T(8,128)S(1)} %get-tuple-element.40.part_k, f32[256,1024]{1,0:T(8,128)S(1)} %get-tuple-element.41.part_v, f32[1024,128]{1,0:T(8,128)S(1)} %shard_map.111.suffix), custom_call_target="tpu_custom_call" | custom-call | tf_op jit(solution)/shard_map/pallas_call | solution.py:44
  104.6 2.1 %shard_map.104 = bf16[256,1024]{1,0:T(8,128)(2,1)} custom-call(s32[2]{0:T(128)S(1)} %compare_select_fusion.at, bf16[1024,4096]{1,0:T(8,128)(2,1)S(1)} %copy-done, bf16[256,1024]{1,0:T(8,128)(2,1)S(1)} %get-tuple-element.36.normed.refs_0_, bf16[256,1024]{1,0:T(8,128)(2,1)S(1)} %collective-permute-done.7.refs_0_, ...), custom_call_target="tpu_custom_call" | custom-call | tf_op jit(solution)/shard_map/pallas_call | solution.py:44
  106.7 2.3 %shard_map.118 = f32[1024,512]{1,0:T(8,128)} custom-call(s32[2]{0:T(128)S(1)} %compare_select_fusion.at, bf16[256,1024]{1,0:T(8,128)(2,1)S(1)} %collective-permute-done.17.refs_0_, bf16[256,1024]{1,0:T(8,128)(2,1)S(1)} %collective-permute-done.18.refs_1_, f32[1024,512]{1,0:T(8,128)S(1)} %shard_map.115.refs_2_, ...), custom_call_target="tpu_custom_call" | custom-call | tf_op jit(solution)/shard_map/pallas_call | solution.py:44
  (54 shorter events, 18.0 us)
Async XLA Ops:
  0.6 1.0 copy-start.1
  1.7 1.0 copy-start.3
  2.7 6.8 %copy-start.6 = (bf16[256,1024]{1,0:T(8,128)(2,1)S(1)}, bf16[256,1024]{1,0:T(8,128)(2,1)}, u32[]{:S(2)}) copy-start(bf16[256,1024]{1,0:T(8,128)(2,1)} %refs_0_.1) | copy-start | bytes 1572868
  2.7 19.4 %copy-start.2 = (bf16[256,1024]{1,0:T(8,128)(2,1)S(1)}, bf16[256,1024]{1,0:T(8,128)(2,1)}, u32[]{:S(2)}) copy-start(bf16[256,1024]{1,0:T(8,128)(2,1)} %k.7) | copy-start | bytes 1572868
  2.7 19.4 %copy-start.4 = (bf16[256,1024]{1,0:T(8,128)(2,1)S(1)}, bf16[256,1024]{1,0:T(8,128)(2,1)}, u32[]{:S(2)}) copy-start(bf16[256,1024]{1,0:T(8,128)(2,1)} %v.7) | copy-start | bytes 1572868
  2.7 19.4 %copy-start.5 = (bf16[256,1024]{1,0:T(8,128)(2,1)S(1)}, bf16[256,1024]{1,0:T(8,128)(2,1)}, u32[]{:S(2)}) copy-start(bf16[256,1024]{1,0:T(8,128)(2,1)} %q.7) | copy-start | bytes 1572868
  3.1 3.2 %collective-permute-start = (f32[1024,128]{1,0:T(8,128)S(1)}, f32[1024,128]{1,0:T(8,128)}, u32[]{:S(2)}, u32[]{:S(2)}) collective-permute-start(f32[1024,128]{1,0:T(8,128)S(1)} %shard_map.93.total), channel_id=1, source_target_pairs={{0,4},{4,0},{8,12},{12,8},{16,20},{20,16},{24,28},{28,24},{1,5},{5... | collective-permute-start | bytes 1572872 | tf_op jit(solution)/shard_map/ppermute | solution.py:219
  3.6 15.4 %collective-permute-start.3 = (bf16[256,1024]{1,0:T(8,128)(2,1)}, bf16[256,1024]{1,0:T(8,128)(2,1)S(1)}, u32[]{:S(2)}, u32[]{:S(2)}) collective-permute-start(bf16[256,1024]{1,0:T(8,128)(2,1)} %refs_0_.1), channel_id=1, source_target_pairs={{0,1},{1,0},{2,3},{3,2},{4,5},{5,4},{6,7},{7,6},{8,9},{9,8},{10,11... | collective-permute-start | bytes 1572872 | tf_op jit(solution)/shard_map/ppermute | solution.py:252
  6.3 23.4 %copy-start = (bf16[1024,4096]{1,0:T(8,128)(2,1)S(1)}, bf16[1024,4096]{1,0:T(8,128)(2,1)}, u32[]{:S(2)}) copy-start(bf16[1024,4096]{1,0:T(8,128)(2,1)} %weight.17) | copy-start | bytes 25165828
  7.6 12.1 %collective-permute-start.1 = (bf16[1024,128]{1,0:T(8,128)(2,1)S(1)}, bf16[1024,128]{1,0:T(8,128)(2,1)S(1)}, u32[]{:S(2)}, u32[]{:S(2)}) collective-permute-start(bf16[1024,128]{1,0:T(8,128)(2,1)S(1)} %get-tuple-element.32), channel_id=1, source_target_pairs={{0,8},{4,12},{8,0},{12,4},{16,24},{20,28},{24,16},{28,20},{1,9},{5... | collective-permute-start | bytes 786440 | tf_op jit(solution)/shard_map/ppermute | solution.py:219
  9.6 13.5 %collective-permute-start.10 = (bf16[256,1024]{1,0:T(8,128)(2,1)S(1)}, bf16[256,1024]{1,0:T(8,128)(2,1)S(1)}, u32[]{:S(2)}, u32[]{:S(2)}) collective-permute-start(bf16[256,1024]{1,0:T(8,128)(2,1)S(1)} %copy-done.6), channel_id=1, source_target_pairs={{1,2},{2,1},{5,6},{6,5},{9,10},{10,9},{13,14},{14,13},{17,18},{18,... | collective-permute-start | bytes 1572872 | tf_op jit(solution)/shard_map/ppermute | solution.py:252
  19.0 11.9 %collective-permute-start.4 = (bf16[256,1024]{1,0:T(8,128)(2,1)S(1)}, bf16[256,1024]{1,0:T(8,128)(2,1)S(1)}, u32[]{:S(2)}, u32[]{:S(2)}) collective-permute-start(bf16[256,1024]{1,0:T(8,128)(2,1)S(1)} %collective-permute-done.3.refs_0_.refs_1_), channel_id=1, source_target_pairs={{1,2},{2,1},{5,6},{6,5},{9,10},{10,9},{13,14},{14,13},{17,18},{18,... | collective-permute-start | bytes 1572872 | tf_op jit(solution)/shard_map/ppermute | solution.py:252
  20.4 8.1 %collective-permute-start.2 = (bf16[1024,128]{1,0:T(8,128)(2,1)S(1)}, bf16[1024,128]{1,0:T(8,128)(2,1)S(1)}, u32[]{:S(2)}, u32[]{:S(2)}) collective-permute-start(bf16[1024,128]{1,0:T(8,128)(2,1)S(1)} %get-tuple-element.35), channel_id=1, source_target_pairs={{0,16},{4,20},{8,24},{12,28},{16,0},{20,4},{24,8},{28,12},{1,17},{... | collective-permute-start | bytes 786440 | tf_op jit(solution)/shard_map/ppermute | solution.py:219
  23.1 18.0 %collective-permute-start.11 = (bf16[256,1024]{1,0:T(8,128)(2,1)S(1)}, bf16[256,1024]{1,0:T(8,128)(2,1)S(1)}, u32[]{:S(2)}, u32[]{:S(2)}) collective-permute-start(bf16[256,1024]{1,0:T(8,128)(2,1)S(1)} %collective-permute-done.10.refs_1_.refs_2_), channel_id=1, source_target_pairs={{1,0},{2,3},{5,4},{6,7},{9,8},{10,11},{13,12},{14,15},{17,16},{18,... | collective-permute-start | bytes 1572872 | tf_op jit(solution)/shard_map/ppermute | solution.py:252
  31.5 19.5 %collective-permute-start.5 = (bf16[256,1024]{1,0:T(8,128)(2,1)S(1)}, bf16[256,1024]{1,0:T(8,128)(2,1)S(1)}, u32[]{:S(2)}, u32[]{:S(2)}) collective-permute-start(bf16[256,1024]{1,0:T(8,128)(2,1)S(1)} %shard_map.99), channel_id=1, source_target_pairs={{1,0},{2,3},{0,1},{3,2},{5,4},{6,7},{4,5},{7,6},{9,8},{10,11},{8,9... | collective-permute-start | bytes 1572872 | tf_op jit(solution)/shard_map/ppermute | solution.py:277
  38.6 16.9 %collective-permute-start.16 = (bf16[256,1024]{1,0:T(8,128)(2,1)S(1)}, bf16[256,1024]{1,0:T(8,128)(2,1)S(1)}, u32[]{:S(2)}, u32[]{:S(2)}) collective-permute-start(bf16[256,1024]{1,0:T(8,128)(2,1)S(1)} %get-tuple-element.36.normed.refs_0_), channel_id=1, source_target_pairs={{0,8},{4,12},{8,0},{12,4},{16,24},{20,28},{24,16},{28,20},{1,9},{5... | collective-permute-start | bytes 1572872 | tf_op jit(solution)/shard_map/ppermute | solution.py:295
  39.4 16.1 %collective-permute-start.15 = (bf16[256,1024]{1,0:T(8,128)(2,1)S(1)}, bf16[256,1024]{1,0:T(8,128)(2,1)S(1)}, u32[]{:S(2)}, u32[]{:S(2)}) collective-permute-start(bf16[256,1024]{1,0:T(8,128)(2,1)S(1)} %get-tuple-element.36.normed.refs_0_), channel_id=1, source_target_pairs={{0,16},{4,20},{8,24},{12,28},{16,0},{20,4},{24,8},{28,12},{1,17},{... | collective-permute-start | bytes 1572872 | tf_op jit(solution)/shard_map/ppermute | solution.py:295
  51.9 14.9 %collective-permute-start.19 = (bf16[256,1024]{1,0:T(8,128)(2,1)S(1)}, bf16[256,1024]{1,0:T(8,128)(2,1)S(1)}, u32[]{:S(2)}, u32[]{:S(2)}) collective-permute-start(bf16[256,1024]{1,0:T(8,128)(2,1)S(1)} %get-tuple-element.53), channel_id=1, source_target_pairs={{0,8},{4,12},{8,0},{12,4},{16,24},{20,28},{24,16},{28,20},{1,9},{5... | collective-permute-start | bytes 1572872 | tf_op jit(solution)/shard_map/ppermute | solution.py:351
  53.5 26.0 %collective-permute-start.20 = (bf16[256,1024]{1,0:T(8,128)(2,1)S(1)}, bf16[256,1024]{1,0:T(8,128)(2,1)S(1)}, u32[]{:S(2)}, u32[]{:S(2)}) collective-permute-start(bf16[256,1024]{1,0:T(8,128)(2,1)S(1)} %get-tuple-element.54), channel_id=1, source_target_pairs={{0,16},{4,20},{8,24},{12,28},{16,0},{20,4},{24,8},{28,12},{1,17},{... | collective-permute-start | bytes 1572872 | tf_op jit(solution)/shard_map/ppermute | solution.py:351
  54.0 28.0 %collective-permute-start.18 = (bf16[256,1024]{1,0:T(8,128)(2,1)S(1)}, bf16[256,1024]{1,0:T(8,128)(2,1)S(1)}, u32[]{:S(2)}, u32[]{:S(2)}) collective-permute-start(bf16[256,1024]{1,0:T(8,128)(2,1)S(1)} %get-tuple-element.51), channel_id=1, source_target_pairs={{0,24},{4,28},{8,16},{12,20},{16,8},{20,12},{24,0},{28,4},{1,25},{... | collective-permute-start | bytes 1572872 | tf_op jit(solution)/shard_map/ppermute | solution.py:351
  56.1 25.9 %collective-permute-start.17 = (bf16[256,1024]{1,0:T(8,128)(2,1)S(1)}, bf16[256,1024]{1,0:T(8,128)(2,1)S(1)}, u32[]{:S(2)}, u32[]{:S(2)}) collective-permute-start(bf16[256,1024]{1,0:T(8,128)(2,1)S(1)} %shard_map.113), channel_id=1, source_target_pairs={{0,8},{4,20},{8,0},{12,28},{16,24},{20,4},{24,16},{28,12},{1,9},{5... | collective-permute-start | bytes 1572872 | tf_op jit(solution)/shard_map/ppermute | solution.py:295
  63.7 19.5 %collective-permute-start.12 = (f32[1024,128]{1,0:T(8,128)S(1)}, f32[1024,128]{1,0:T(8,128)S(1)}, u32[]{:S(2)}, u32[]{:S(2)}) collective-permute-start(f32[1024,128]{1,0:T(8,128)S(1)} %get-tuple-element.42.total), channel_id=1, source_target_pairs={{0,4},{4,0},{8,12},{12,8},{16,20},{20,16},{24,28},{28,24},{1,5},{5... | collective-permute-start | bytes 1572872 | tf_op jit(solution)/shard_map/ppermute | solution.py:219
  66.8 18.1 %collective-permute-start.8 = (bf16[256,1024]{1,0:T(8,128)(2,1)S(1)}, bf16[256,1024]{1,0:T(8,128)(2,1)S(1)}, u32[]{:S(2)}, u32[]{:S(2)}) collective-permute-start(bf16[256,1024]{1,0:T(8,128)(2,1)S(1)} %shard_map.102), channel_id=1, source_target_pairs={{0,1},{3,2},{4,5},{7,6},{8,9},{11,10},{12,13},{15,14},{16,17},{19,... | collective-permute-start | bytes 1572872 | tf_op jit(solution)/shard_map/ppermute | solution.py:269
  79.6 7.4 %collective-permute-start.6 = (bf16[256,1024]{1,0:T(8,128)(2,1)S(1)}, bf16[256,1024]{1,0:T(8,128)(2,1)S(1)}, u32[]{:S(2)}, u32[]{:S(2)}) collective-permute-start(bf16[256,1024]{1,0:T(8,128)(2,1)S(1)} %shard_map.100), channel_id=1, source_target_pairs={{2,1},{1,2},{6,5},{5,6},{10,9},{9,10},{14,13},{13,14},{18,17},{17,... | collective-permute-start | bytes 1572872 | tf_op jit(solution)/shard_map/ppermute | solution.py:269
  83.1 23.7 %collective-permute-start.21 = (bf16[1024,512]{1,0:T(8,128)(2,1)S(1)}, bf16[1024,512]{1,0:T(8,128)(2,1)S(1)}, u32[]{:S(2)}, u32[]{:S(2)}) collective-permute-start(bf16[1024,512]{1,0:T(8,128)(2,1)S(1)} %shard_map.117), channel_id=1, source_target_pairs={{0,4},{4,0},{8,12},{12,8},{16,20},{20,16},{24,28},{28,24},{1,5},{5... | collective-permute-start | bytes 3145736 | tf_op jit(solution)/shard_map/ppermute | solution.py:382
  84.0 8.6 %collective-permute-start.13 = (bf16[1024,128]{1,0:T(8,128)(2,1)S(1)}, bf16[1024,128]{1,0:T(8,128)(2,1)S(1)}, u32[]{:S(2)}, u32[]{:S(2)}) collective-permute-start(bf16[1024,128]{1,0:T(8,128)(2,1)S(1)} %get-tuple-element.45), channel_id=1, source_target_pairs={{0,8},{4,12},{8,0},{12,4},{16,24},{20,28},{24,16},{28,20},{1,9},{5... | collective-permute-start | bytes 786440 | tf_op jit(solution)/shard_map/ppermute | solution.py:219
  86.2 17.3 %collective-permute-start.9 = (bf16[256,1024]{1,0:T(8,128)(2,1)S(1)}, bf16[256,1024]{1,0:T(8,128)(2,1)S(1)}, u32[]{:S(2)}, u32[]{:S(2)}) collective-permute-start(bf16[256,1024]{1,0:T(8,128)(2,1)S(1)} %shard_map.103), channel_id=1, source_target_pairs={{2,1},{1,2},{6,5},{5,6},{10,9},{9,10},{14,13},{13,14},{18,17},{17,... | collective-permute-start | bytes 1572872 | tf_op jit(solution)/shard_map/ppermute | solution.py:269
  88.2 16.4 %collective-permute-start.7 = (bf16[256,1024]{1,0:T(8,128)(2,1)S(1)}, bf16[256,1024]{1,0:T(8,128)(2,1)S(1)}, u32[]{:S(2)}, u32[]{:S(2)}) collective-permute-start(bf16[256,1024]{1,0:T(8,128)(2,1)S(1)} %shard_map.101), channel_id=1, source_target_pairs={{1,0},{0,1},{3,2},{2,3},{5,4},{4,5},{7,6},{6,7},{9,8},{8,9},{11,10... | collective-permute-start | bytes 1572872 | tf_op jit(solution)/shard_map/ppermute | solution.py:269
  93.3 7.9 %collective-permute-start.14 = (bf16[1024,128]{1,0:T(8,128)(2,1)S(1)}, bf16[1024,128]{1,0:T(8,128)(2,1)S(1)}, u32[]{:S(2)}, u32[]{:S(2)}) collective-permute-start(bf16[1024,128]{1,0:T(8,128)(2,1)S(1)} %get-tuple-element.48), channel_id=1, source_target_pairs={{0,16},{4,20},{8,24},{12,28},{16,0},{20,4},{24,8},{28,12},{1,17},{... | collective-permute-start | bytes 786440 | tf_op jit(solution)/shard_map/ppermute | solution.py:219
